TPU v7x, 768 devices: a whole 4x8x12 slice. The times are simulated.
768 devices in a mesh: lon: 24 (over x_lo, z), lat: 32 (over x_hi, y, core).
Axes of the slice: x: 4 (x_hi: 2, x_lo: 2; x = x_hi * 2 + x_lo), y: 8, z: 12, core: 2. Of those that a mesh axis runs over, the one named last changes fastest.
Arguments:
- free_elevation: float32 [512, 6144], P('lat', 'lon'), may hold values from -3 to 3
- zonal_volume_carriage: float32 [512, 6144], P('lat', 'lon'), may hold values from -2 to 2
- meridional_volume_carriage: float32 [512, 6144], P('lat', 'lon'), may hold values from -2 to 2
- thermal_field: float32 [60, 512, 6144], P(None, 'lat', 'lon'), may hold values from -6 to 6
- flooded_strata_number: int32 [512, 6144], P('lat', 'lon'), may hold values from 0 to 60, as said below
- aerial_exchanges: float32 [5, 256, 3072], P(None, 'lat', 'lon'), may hold values from -6 to 6
- aerial_terrain_flags: int32 [256, 3072], P('lat', 'lon'), may hold values 0 or 1
- donor_tile_number: int32 [4, 512, 48], P(None, 'lat', 'lon'), may hold values from 0 to 23
- donor_point_number: int32 [4, 512, 6144], P(None, 'lat', 'lon'), may hold values from 0 to 127
- pairing_coefficients: float32 [4, 512, 6144], P(None, 'lat', 'lon'), may hold values from 0 to 0.5
Outputs:
- advanced_elevation: float32 [512, 6144], P('lat', 'lon')
- transport_x_next: float32 [512, 6144], P('lat', 'lon')
- transport_y_next: float32 [512, 6144], P('lat', 'lon')
- advanced_thermal_field: float32 [60, 512, 6144], P(None, 'lat', 'lon')
- marine_skin_condition: float32 [4, 256, 3072], P(None, 'lat', 'lon')
Inputs may be any that keep to these rules, and one draw needn't show every extreme that they name: flooded_strata_number is 0 on land; wet columns hold 1 to 60 levels. donor_tile_number // 8 - 1 is the source tile's offset in latitude and donor_tile_number mod 8 the source block (row) within it; the longitude tile is the target's.
All inputs are finite; a program needn't handle non-finite values. No bound on the sum of `aerial_terrain_flags` on one device may be relied on, other than what follows from the above.
Results may differ from a plain program's by a relative error of at most 0.0003.
Values sent between devices are 32-bit elements; how exact they have to be, the bound alone decides.
A program may use at most 32 MiB of HBM per device.

v0:
```python
import math

import jax
import jax.numpy as jnp
from jax import lax
from jax.sharding import PartitionSpec as P

SUBS = 3


grav_step = 0.6
height_step = 0.6
wind_step = 0.5
fresh_step = 0.5
mixing_fourth = 0.02
advect_coef = 0.1
diapycnal_diffusion = 0.2
heat_gain = 0.3
light_gain = 0.3
light_decay = 8.0
depth_floor = 0.25
area_floor = 1.0


def padded_2(block, sides, width, periodic):
    for axis, dim in sides:
        count = lax.axis_size(axis)
        forward = [(i, i + 1) for i in range(count - 1)]
        if periodic:
            forward.append((count - 1, 0))
        backward = [(target, source) for source, target in forward]
        low = lax.ppermute(
            lax.slice_in_dim(block, block.shape[dim] - width, None, axis=dim), axis, forward
        )
        high = lax.ppermute(lax.slice_in_dim(block, 0, width, axis=dim), axis, backward)
        block = jnp.concatenate([low, block, high], axis=dim)
    return block


def shifted(array, axis, by):
    length = lax.axis_size(axis)
    pairs = [(i, i + by) for i in range(length) if 0 <= i + by < length]
    return lax.ppermute(array, axis, pairs)


def column_depth(stratum_tally_sheet, stratum_entries):
    scale = 1.0 / (2.0 * stratum_entries)
    return stratum_tally_sheet * scale + stratum_tally_sheet * (stratum_tally_sheet - 1.0) * (
        scale / stratum_entries
    )


def barotropic_step(planes, stratum_entries):
    height = planes[0]
    zonal_velocity = planes[1]
    meridional_velocity = planes[2]
    stratum_tally_sheet = planes[3]
    wind_east = planes[4]
    wind_north = planes[5]
    fresh_water = planes[6]
    stratum_thicknesses = column_depth(stratum_tally_sheet, stratum_entries)
    lone_flooded_point = (stratum_tally_sheet > 0.5).astype(jnp.float32)
    east_face = lone_flooded_point[1:-1, :-1] * lone_flooded_point[1:-1, 1:]
    east_depth = jnp.minimum(stratum_thicknesses[1:-1, :-1], stratum_thicknesses[1:-1, 1:])
    east_flow = east_face * (
        zonal_velocity[1:-1, :-1]
        - grav_step * east_depth * (height[1:-1, 1:] - height[1:-1, :-1])
        + wind_step * wind_east[1:-1, :-1]
    )
    north_face = lone_flooded_point[:-1, 1:-1] * lone_flooded_point[1:, 1:-1]
    north_depth = jnp.minimum(stratum_thicknesses[:-1, 1:-1], stratum_thicknesses[1:, 1:-1])
    north_flow = north_face * (
        meridional_velocity[:-1, 1:-1]
        - grav_step * north_depth * (height[1:, 1:-1] - height[:-1, 1:-1])
        + wind_step * wind_north[:-1, 1:-1]
    )
    spread = east_flow[:, 1:] - east_flow[:, :-1] + north_flow[1:, :] - north_flow[:-1, :]
    inner_wet = lone_flooded_point[1:-1, 1:-1]
    new_height = height[1:-1, 1:-1] + inner_wet * (
        fresh_step * fresh_water[1:-1, 1:-1] - height_step * spread
    )
    return jnp.stack(
        [
            new_height,
            east_flow[:, 1:],
            north_flow[1:, :],
            stratum_tally_sheet[1:-1, 1:-1],
            wind_east[1:-1, 1:-1],
            wind_north[1:-1, 1:-1],
            fresh_water[1:-1, 1:-1],
        ]
    )


def face_masks(count_border, level_order):
    east_open = (level_order < jnp.minimum(count_border[:, :-1], count_border[:, 1:])).astype(
        jnp.float32
    )
    north_open = (level_order < jnp.minimum(count_border[:-1, :], count_border[1:, :])).astype(
        jnp.float32
    )
    return (east_open, north_open)


def laplace(field, count_border, level_order):
    east_open, north_open = face_masks(count_border, level_order)
    flux_east = east_open * (field[..., 1:] - field[..., :-1])
    flux_north = north_open * (field[..., 1:, :] - field[..., :-1, :])
    return (
        flux_east[..., 1:-1, 1:]
        - flux_east[..., 1:-1, :-1]
        + flux_north[..., 1:, 1:-1]
        - flux_north[..., :-1, 1:-1]
    )


def face_speeds(stratum_thicknesses, east_border, north_border):
    speed_east = east_border[:, :-1] / jnp.maximum(
        jnp.minimum(stratum_thicknesses[:, :-1], stratum_thicknesses[:, 1:]), depth_floor
    )
    speed_north = north_border[:-1, :] / jnp.maximum(
        jnp.minimum(stratum_thicknesses[:-1, :], stratum_thicknesses[1:, :]), depth_floor
    )
    return (speed_east, speed_north)


def horizontal_tendency(
    temp_border, lap_border, count_border, speed_east, speed_north, level_order
):
    mixing = laplace(lap_border, count_border, level_order)
    east_open, north_open = face_masks(count_border, level_order)
    carry_east = east_open * speed_east * 0.5 * (temp_border[..., 1:] + temp_border[..., :-1])
    carry_north = (
        north_open * speed_north * 0.5 * (temp_border[..., 1:, :] + temp_border[..., :-1, :])
    )
    advect = (
        carry_east[..., 1:-1, 1:]
        - carry_east[..., 1:-1, :-1]
        + carry_north[..., 1:, 1:-1]
        - carry_north[..., :-1, 1:-1]
    )
    return -advect_coef * advect - mixing_fourth * mixing


def profile_change_rate(
    thermal_field,
    lateral_contribution,
    stratum_tally_sheet,
    boundary_thermal_exchange,
    solar_radiation,
    stratum_entries,
):
    level_order = jnp.arange(stratum_entries, dtype=jnp.float32)[:, None, None]
    flooded_point_flags = (level_order < stratum_tally_sheet).astype(jnp.float32)
    beneath_stratum_flooded = (level_order + 1.0 < stratum_tally_sheet).astype(jnp.float32)
    sinking_exchange = beneath_stratum_flooded[:-1] * (thermal_field[1:] - thermal_field[:-1])
    blank_sheet = jnp.zeros_like(thermal_field[:1])
    radial_contribution = jnp.concatenate([sinking_exchange, blank_sheet]) - jnp.concatenate(
        [blank_sheet, sinking_exchange]
    )
    absorb = jnp.exp(-level_order / light_decay) * (1.0 - math.exp(-1.0 / light_decay))
    top_level = (level_order < 0.5).astype(jnp.float32)
    donor_entries = (
        light_gain * absorb * solar_radiation + heat_gain * boundary_thermal_exchange * top_level
    )
    return thermal_field + flooded_point_flags * (
        diapycnal_diffusion * radial_contribution + lateral_contribution + donor_entries
    )


def column_onehot(columns, rows, blocks, width):
    lanes = lax.broadcasted_iota(jnp.int32, (1, 1, 1, width), 3)
    return (columns.reshape(rows, blocks, width)[..., None] == lanes).astype(jnp.float32)


def regrid_forward(padded, donor_tile_number, donor_point_number, weight):
    nflux, table_rows, width = padded.shape
    links, rows, blocks = donor_tile_number.shape
    running = jnp.zeros((nflux, rows, blocks * width), jnp.float32)
    for link_index in range(links):
        picked = jnp.take(padded, donor_tile_number[link_index], axis=1)
        onehot = column_onehot(donor_point_number[link_index], rows, blocks, width)
        chosen = jnp.einsum("rbjc,frbc->frbj", onehot, picked, precision=lax.Precision.HIGHEST)
        running = running + chosen.reshape(nflux, rows, blocks * width) * weight[link_index][None]
    return running


def regrid_back(values, donor_tile_number, donor_point_number, weight, table_rows):
    planes = values.shape[0]
    links, rows, blocks = donor_tile_number.shape
    width = values.shape[2] // blocks
    targets = lax.broadcasted_iota(jnp.int32, (1, 1, table_rows), 2)
    table = jnp.zeros((planes, table_rows, width), jnp.float32)
    for link_index in range(links):
        shares = (values * weight[link_index][None]).reshape(planes, rows, blocks, width)
        onehot = column_onehot(donor_point_number[link_index], rows, blocks, width)
        by_cell = jnp.einsum("rbjc,srbj->srbc", onehot, shares, precision=lax.Precision.HIGHEST)
        row_hot = (donor_tile_number[link_index][..., None] == targets).astype(jnp.float32)
        table = table + jnp.einsum(
            "rbt,srbc->stc", row_hot, by_cell, precision=lax.Precision.HIGHEST
        )
    return table


def clear_poles(extended, plane_index, width):
    row_total = extended.shape[1]
    band_index = lax.axis_index("lat")
    band_total = lax.axis_size("lat")
    row_ids = lax.broadcasted_iota(jnp.int32, (row_total, 1), 0)
    south_rim = (band_index == 0) & (row_ids < width)
    north_rim = (band_index == band_total - 1) & (row_ids >= row_total - width)
    keep_rows = jnp.where(south_rim | north_rim, 0.0, 1.0)
    return extended.at[plane_index].multiply(keep_rows)


def shards(
    free_elevation,
    zonal_volume_carriage,
    meridional_volume_carriage,
    thermal_field,
    flooded_strata_number,
    aerial_exchanges,
    aerial_terrain_flags,
    donor_tile_number,
    donor_point_number,
    pairing_coefficients,
):
    stratum_entries = thermal_field.shape[0]
    band_rows = aerial_exchanges.shape[1]
    open_sea = (1 - aerial_terrain_flags).astype(jnp.float32)
    masked = aerial_exchanges * open_sea[None]
    padded = padded_2(masked, (("lat", 1),), band_rows, False)
    boundary_driving = regrid_forward(
        padded, donor_tile_number, donor_point_number, pairing_coefficients
    )
    stratum_tally_sheet = flooded_strata_number.astype(jnp.float32)
    planes = jnp.stack(
        [
            free_elevation,
            zonal_volume_carriage,
            meridional_volume_carriage,
            stratum_tally_sheet,
            boundary_driving[0],
            boundary_driving[1],
            boundary_driving[4],
        ]
    )
    present_scalar_field = planes
    for cycle_index in range(SUBS):
        extended = padded_2(present_scalar_field, (("lon", 2), ("lat", 1)), 1, True)
        present_scalar_field = barotropic_step(clear_poles(extended, 3, 1), stratum_entries)
    advanced_elevation = present_scalar_field[0]
    zonal_velocity = present_scalar_field[1]
    meridional_velocity = present_scalar_field[2]
    level_order = jnp.arange(stratum_entries, dtype=jnp.float32)[:, None, None]
    scalar_strata = jnp.concatenate(
        [thermal_field, present_scalar_field[3:4], present_scalar_field[1:3]]
    )
    bordered = padded_2(scalar_strata, (("lon", 2), ("lat", 1)), 1, True)
    bordered = clear_poles(bordered, stratum_entries, 1)
    inner_lap = laplace(bordered[:stratum_entries], bordered[stratum_entries], level_order)
    lap_border = padded_2(inner_lap, (("lon", 2), ("lat", 1)), 1, True)
    count_border = bordered[stratum_entries]
    depth_border = column_depth(count_border, stratum_entries)
    speed_east, speed_north = face_speeds(
        depth_border, bordered[stratum_entries + 1], bordered[stratum_entries + 2]
    )
    lateral_contribution = horizontal_tendency(
        bordered[:stratum_entries], lap_border, count_border, speed_east, speed_north, level_order
    )
    advanced_thermal_field = profile_change_rate(
        thermal_field,
        lateral_contribution,
        stratum_tally_sheet,
        boundary_driving[2],
        boundary_driving[3],
        stratum_entries,
    )
    lone_flooded_point = (stratum_tally_sheet > 0.5).astype(jnp.float32)
    stratum_thicknesses = jnp.maximum(depth_border[1:-1, 1:-1], depth_floor)
    uppermost_stratum = (
        jnp.stack(
            [
                advanced_thermal_field[0],
                advanced_elevation,
                zonal_velocity / stratum_thicknesses,
                meridional_velocity / stratum_thicknesses,
            ]
        )
        * lone_flooded_point[None]
    )
    values = jnp.concatenate(
        [uppermost_stratum * lone_flooded_point[None], lone_flooded_point[None]]
    )
    table = regrid_back(
        values, donor_tile_number, donor_point_number, pairing_coefficients, 3 * band_rows
    )
    link_sums = table[:-1]
    link_area = table[-1]
    from_north = shifted((link_sums[:, :band_rows], link_area[:band_rows]), "lat", -1)
    from_south = shifted((link_sums[:, 2 * band_rows :], link_area[2 * band_rows :]), "lat", 1)
    merged_sums = link_sums[:, band_rows : 2 * band_rows] + from_north[0] + from_south[0]
    merged_area = link_area[band_rows : 2 * band_rows] + from_north[1] + from_south[1]
    marine_skin_condition = (
        open_sea[None] * merged_sums / jnp.maximum(merged_area, area_floor)[None]
    )
    return (
        advanced_elevation,
        zonal_velocity,
        meridional_velocity,
        advanced_thermal_field,
        marine_skin_condition,
    )


def solution(mesh):
    placed = (
        P("lat", "lon"),
        P("lat", "lon"),
        P("lat", "lon"),
        P(None, "lat", "lon"),
        P("lat", "lon"),
        P(None, "lat", "lon"),
        P("lat", "lon"),
        P(None, "lat", "lon"),
        P(None, "lat", "lon"),
        P(None, "lat", "lon"),
    )
    return jax.shard_map(
        shards,
        mesh=mesh,
        in_specs=placed,
        out_specs=(
            P("lat", "lon"),
            P("lat", "lon"),
            P("lat", "lon"),
            P(None, "lat", "lon"),
            P(None, "lat", "lon"),
        ),
        check_vma=False,
    )
```

profile of v0, /device:TPU:57, one launch (start us, length us, event | category | flops | bytes accessed | tf_op | source)
XLA Modules:
  0.0 216.7 jit_solution(704607271298175615)
XLA Ops:
  2.1 2.6 %collective-permute-start.1 = (f32[5,8,128]{2,0,1:T(8,128)S(1)}, f32[5,8,128]{2,0,1:T(8,128)S(1)}, u32[]{:S(2)}, u32[]{:S(2)}) collective-permute-start(f32[5,8,128]{2,0,1:T(8,128)S(1)} %copy_multiply_fusion), channel_id=1, source_target_pairs={{1,0},{2,1},{3,2},{4,3},{5,4},{6,5},{7,6},{8,7},{9,8},{10,9},{11,1... | collective-permute-start | bytes 61448 | tf_op jit(solution)/shard_map/ppermute | solution.py:35
  4.7 6.6 %collective-permute-start = (f32[5,8,128]{2,0,1:T(8,128)S(1)}, f32[5,8,128]{2,0,1:T(8,128)S(1)}, u32[]{:S(2)}, u32[]{:S(2)}) collective-permute-start(f32[5,8,128]{2,0,1:T(8,128)S(1)} %copy_multiply_fusion), channel_id=1, source_target_pairs={{0,1},{1,2},{2,3},{3,4},{4,5},{5,6},{6,7},{7,8},{8,9},{9,10},{10,1... | collective-permute-start | bytes 61448 | tf_op jit(solution)/shard_map/ppermute | solution.py:32
  19.0 2.4 %fusion.13 = f32[5,16,2,128]{3,0,2,1:T(8,128)S(1)} fusion(s32[16,2,128]{2,1,0:T(2,128)S(1)} %eq.72, f32[16,2,5,128]{3,2,1,0:T(8,128)S(1)} %bitcast.244, pred[16,2]{1,0:T(8,128)(4,1)S(1)} %copy.37), kind=kOutput, calls=%fused_computation.43 | convolution fusion | flops 32002048 | bytes 180256 | tf_op jit(solution)/shard_map/rbjc,frbc->frbj/dot_general | solution.py:183
  22.2 2.4 %fusion.12 = f32[5,16,2,128]{3,0,2,1:T(8,128)S(1)} fusion(s32[16,2,128]{2,1,0:T(2,128)S(1)} %eq.68, f32[16,2,5,128]{3,2,1,0:T(8,128)S(1)} %bitcast.245, pred[16,2]{1,0:T(8,128)(4,1)S(1)} %copy.34), kind=kOutput, calls=%fused_computation.42 | convolution fusion | flops 32002048 | bytes 180256 | tf_op jit(solution)/shard_map/rbjc,frbc->frbj/dot_general | solution.py:183
  25.3 2.4 %fusion.11 = f32[5,16,2,128]{3,0,2,1:T(8,128)S(1)} fusion(s32[16,2,128]{2,1,0:T(2,128)S(1)} %eq.64, f32[16,2,5,128]{3,2,1,0:T(8,128)S(1)} %bitcast.246, pred[16,2]{1,0:T(8,128)(4,1)S(1)} %copy.31), kind=kOutput, calls=%fused_computation.41 | convolution fusion | flops 32002048 | bytes 180256 | tf_op jit(solution)/shard_map/rbjc,frbc->frbj/dot_general | solution.py:183
  28.5 2.4 %fusion.10 = f32[5,16,2,128]{3,0,2,1:T(8,128)S(1)} fusion(s32[16,2,128]{2,1,0:T(2,128)S(1)} %eq.60, f32[16,2,5,128]{3,2,1,0:T(8,128)S(1)} %bitcast.243, pred[16,2]{1,0:T(8,128)(4,1)S(1)} %copy.27), kind=kOutput, calls=%fused_computation.40 | convolution fusion | flops 32002048 | bytes 180256 | tf_op jit(solution)/shard_map/rbjc,frbc->frbj/dot_general | solution.py:183
  31.7 15.2 %collective-permute-start.3 = (f32[7,16,1]{2,1,0:T(8,128)S(1)}, f32[7,16,1]{2,1,0:T(8,128)S(1)}, u32[]{:S(2)}, u32[]{:S(2)}) collective-permute-start(f32[7,16,1]{2,1,0:T(8,128)S(1)} %get-tuple-element.104), channel_id=1, source_target_pairs={{32,0},{64,32},{96,64},{128,96},{160,128},{192,160},{224,192},{256... | collective-permute-start | bytes 1352 | tf_op jit(solution)/shard_map/ppermute | solution.py:35
  47.0 1.9 collective-permute-start.2
  48.9 5.1 %collective-permute-done.2 = f32[7,16,1]{2,1,0:T(8,128)S(1)} collective-permute-done((f32[7,16,1]{2,1,0:T(8,128)S(1)}, f32[7,16,1]{2,1,0:T(8,128)S(1)}, u32[]{:S(2)}, u32[]{:S(2)}) %collective-permute-start.2) | collective-permute-done | bytes 480 | tf_op jit(solution)/shard_map/ppermute | solution.py:32
  54.1 1.9 collective-permute-start.5
  56.1 7.3 %collective-permute-start.4 = (f32[7,1,258]{2,1,0:T(1,128)S(1)}, f32[7,1,258]{2,1,0:T(1,128)S(1)}, u32[]{:S(2)}, u32[]{:S(2)}) collective-permute-start(f32[7,1,258]{2,1,0:T(1,128)S(1)} %get-tuple-element.97), channel_id=1, source_target_pairs={{0,1},{1,2},{2,3},{3,4},{4,5},{5,6},{6,7},{7,8},{8,9},{9,10},{10,1... | collective-permute-start | bytes 21680 | tf_op jit(solution)/shard_map/ppermute | solution.py:32
  65.2 1.9 collective-permute-start.7
  67.1 3.4 %collective-permute-start.6 = (f32[7,16,1]{2,1,0:T(8,128)S(1)}, f32[7,16,1]{2,1,0:T(8,128)S(1)}, u32[]{:S(2)}, u32[]{:S(2)}) collective-permute-start(f32[7,16,1]{2,1,0:T(8,128)S(1)} %get-tuple-element.101), channel_id=1, source_target_pairs={{0,32},{32,64},{64,96},{96,128},{128,160},{160,192},{192,224},{224... | collective-permute-start | bytes 1352 | tf_op jit(solution)/shard_map/ppermute | solution.py:32
  70.5 3.6 %collective-permute-done.6 = f32[7,16,1]{2,1,0:T(8,128)S(1)} collective-permute-done((f32[7,16,1]{2,1,0:T(8,128)S(1)}, f32[7,16,1]{2,1,0:T(8,128)S(1)}, u32[]{:S(2)}, u32[]{:S(2)}) %collective-permute-start.6) | collective-permute-done | bytes 480 | tf_op jit(solution)/shard_map/ppermute | solution.py:32
  74.3 1.9 collective-permute-start.9
  76.2 9.5 %collective-permute-start.8 = (f32[7,1,258]{2,1,0:T(1,128)S(1)}, f32[7,1,258]{2,1,0:T(1,128)S(1)}, u32[]{:S(2)}, u32[]{:S(2)}) collective-permute-start(f32[7,1,258]{2,1,0:T(1,128)S(1)} %get-tuple-element.95), channel_id=1, source_target_pairs={{0,1},{1,2},{2,3},{3,4},{4,5},{5,6},{6,7},{7,8},{8,9},{9,10},{10,1... | collective-permute-start | bytes 21680 | tf_op jit(solution)/shard_map/ppermute | solution.py:32
  85.7 1.1 subtract_select_fusion.2
  87.9 1.9 collective-permute-start.11
  89.8 3.4 %collective-permute-start.10 = (f32[7,16,1]{2,1,0:T(8,128)S(1)}, f32[7,16,1]{2,1,0:T(8,128)S(1)}, u32[]{:S(2)}, u32[]{:S(2)}) collective-permute-start(f32[7,16,1]{2,1,0:T(8,128)S(1)} %get-tuple-element.99), channel_id=1, source_target_pairs={{0,32},{32,64},{64,96},{96,128},{128,160},{160,192},{192,224},{224... | collective-permute-start | bytes 1352 | tf_op jit(solution)/shard_map/ppermute | solution.py:32
  93.2 3.6 %collective-permute-done.10 = f32[7,16,1]{2,1,0:T(8,128)S(1)} collective-permute-done((f32[7,16,1]{2,1,0:T(8,128)S(1)}, f32[7,16,1]{2,1,0:T(8,128)S(1)}, u32[]{:S(2)}, u32[]{:S(2)}) %collective-permute-start.10) | collective-permute-done | bytes 480 | tf_op jit(solution)/shard_map/ppermute | solution.py:32
  97.0 1.9 collective-permute-start.13
  98.9 8.6 %collective-permute-start.12 = (f32[7,1,258]{2,1,0:T(1,128)S(1)}, f32[7,1,258]{2,1,0:T(1,128)S(1)}, u32[]{:S(2)}, u32[]{:S(2)}) collective-permute-start(f32[7,1,258]{2,1,0:T(1,128)S(1)} %get-tuple-element.93), channel_id=1, source_target_pairs={{0,1},{1,2},{2,3},{3,4},{4,5},{5,6},{6,7},{7,8},{8,9},{9,10},{10,1... | collective-permute-start | bytes 21680 | tf_op jit(solution)/shard_map/ppermute | solution.py:32
  109.3 1.9 collective-permute-start.15
  111.3 3.4 %collective-permute-start.14 = (f32[63,16,1]{2,1,0:T(8,128)S(1)}, f32[63,16,1]{2,1,0:T(8,128)S(1)}, u32[]{:S(2)}, u32[]{:S(2)}) collective-permute-start(f32[63,16,1]{2,1,0:T(8,128)S(1)} %get-tuple-element.71), channel_id=1, source_target_pairs={{0,32},{32,64},{64,96},{96,128},{128,160},{160,192},{192,224},{224... | collective-permute-start | bytes 12104 | tf_op jit(solution)/shard_map/ppermute | solution.py:32
  119.2 4.0 %collective-permute-done.14 = f32[63,16,1]{2,1,0:T(8,128)S(1)} collective-permute-done((f32[63,16,1]{2,1,0:T(8,128)S(1)}, f32[63,16,1]{2,1,0:T(8,128)S(1)}, u32[]{:S(2)}, u32[]{:S(2)}) %collective-permute-start.14) | collective-permute-done | bytes 4064 | tf_op jit(solution)/shard_map/ppermute | solution.py:32
  123.8 1.9 collective-permute-start.17
  125.7 9.1 %collective-permute-start.16 = (f32[63,1,258]{2,1,0:T(1,128)S(1)}, f32[63,1,258]{2,1,0:T(1,128)S(1)}, u32[]{:S(2)}, u32[]{:S(2)}) collective-permute-start(f32[63,1,258]{2,1,0:T(1,128)S(1)} %get-tuple-element.67), channel_id=1, source_target_pairs={{0,1},{1,2},{2,3},{3,4},{4,5},{5,6},{6,7},{7,8},{8,9},{9,10},{10,1... | collective-permute-start | bytes 195056 | tf_op jit(solution)/shard_map/ppermute | solution.py:32
  137.6 2.0 add_multiply_fusion.1
  139.6 5.9 %subtract_select_fusion = f32[60,17,258]{2,1,0:T(8,128)S(1)} fusion(f32[17,258]{1,0:T(8,128)S(1)} %fusion.72, f32[63,1,258]{2,1,0:T(1,128)S(1)} %collective-permute-done.17, f32[63,16,1]{2,1,0:T(8,128)S(1)} %collective-permute-done.15, f32[1,16,256]{2,1,0:T(8,128)S(1)} %bitcast.239, f32[1,16,256]{2,1,0:T(8,128)S(1)} %bitcast.233, ...), kind=kLoop, calls=%fused_computation.22 | loop fusion | flops 3947400 | bytes 2240472 | tf_op jit(solution)/shard_map/mul | solution.py:108
  146.6 1.9 collective-permute-start.19
  148.6 3.4 %collective-permute-start.18 = (f32[60,16,1]{2,1,0:T(8,128)S(1)}, f32[60,16,1]{2,1,0:T(8,128)S(1)}, u32[]{:S(2)}, u32[]{:S(2)}) collective-permute-start(f32[60,16,1]{2,1,0:T(8,128)S(1)} %get-tuple-element.73), channel_id=1, source_target_pairs={{0,32},{32,64},{64,96},{96,128},{128,160},{160,192},{192,224},{224... | collective-permute-start | bytes 11528 | tf_op jit(solution)/shard_map/ppermute | solution.py:32
  152.1 7.0 %add_multiply_fusion = f32[60,17,258]{2,1,0:T(8,128)} fusion(f32[17,258]{1,0:T(8,128)S(1)} %fusion.71, f32[17,258]{1,0:T(8,128)S(1)} %fusion.72, f32[63,1,258]{2,1,0:T(1,128)S(1)} %copy-done.12, f32[63,16,1]{2,1,0:T(8,128)S(1)} %collective-permute-done.15, f32[1,16,256]{2,1,0:T(8,128)S(1)} %bitcast.241, f32[1,16,256]{2,1,0:T(8,128)S(1)} %bitcast.235, ...), kind=kLoop, calls=%fused_computation.24 | loop fusion | flops 4473720 | bytes 2258016 | tf_op jit(solution)/shard_map/mul | solution.py:134
  159.0 1.2 collective-permute-done.18
  161.6 1.9 collective-permute-start.21
  163.6 9.3 %collective-permute-start.20 = (f32[60,1,258]{2,1,0:T(1,128)S(1)}, f32[60,1,258]{2,1,0:T(1,128)S(1)}, u32[]{:S(2)}, u32[]{:S(2)}) collective-permute-start(f32[60,1,258]{2,1,0:T(1,128)S(1)} %get-tuple-element.69), channel_id=1, source_target_pairs={{0,1},{1,2},{2,3},{3,4},{4,5},{5,6},{6,7},{7,8},{8,9},{9,10},{10,1... | collective-permute-start | bytes 185768 | tf_op jit(solution)/shard_map/ppermute | solution.py:32
  173.0 1.2 collective-permute-done.20
  174.2 1.9 pad_maximum_fusion.13
  177.2 1.4 fusion.1
  179.3 1.9 fusion.31
  181.6 1.8 fusion.8
  183.5 1.8 fusion.6
  185.3 1.8 fusion.4
  187.1 1.8 fusion.2
  190.2 7.9 %collective-permute-start.25 = (f32[8,128]{1,0:T(8,128)S(1)}, f32[8,128]{1,0:T(8,128)S(1)}, u32[]{:S(2)}, u32[]{:S(2)}) collective-permute-start(f32[8,128]{1,0:T(8,128)S(1)} %get-tuple-element.125), channel_id=1, source_target_pairs={{0,1},{1,2},{2,3},{3,4},{4,5},{5,6},{6,7},{7,8},{8,9},{9,10},{10,1... | collective-permute-start | bytes 12296 | tf_op jit(solution)/shard_map/ppermute | solution.py:43
  198.2 1.9 collective-permute-start.24
  200.1 7.3 %collective-permute-start.23 = (f32[4,8,128]{2,1,0:T(8,128)S(1)}, f32[4,8,128]{2,1,0:T(8,128)S(1)}, u32[]{:S(2)}, u32[]{:S(2)}) collective-permute-start(f32[4,8,128]{2,1,0:T(8,128)S(1)} %get-tuple-element.127), channel_id=1, source_target_pairs={{0,1},{1,2},{2,3},{3,4},{4,5},{5,6},{6,7},{7,8},{8,9},{9,10},{10,1... | collective-permute-start | bytes 49160 | tf_op jit(solution)/shard_map/ppermute | solution.py:43
  207.4 1.9 collective-permute-start.22
  209.3 6.7 %collective-permute-done.22 = f32[4,8,128]{2,1,0:T(8,128)S(1)} collective-permute-done((f32[4,8,128]{2,1,0:T(8,128)S(1)}, f32[4,8,128]{2,1,0:T(8,128)S(1)}, u32[]{:S(2)}, u32[]{:S(2)}) %collective-permute-start.22) | collective-permute-done | bytes 16416 | tf_op jit(solution)/shard_map/ppermute | solution.py:43
  (240 shorter events, 31.2 us)
Async XLA Ops:
  1.3 10.7 %copy-start.28 = (f32[8,128]{1,0:T(8,128)}, f32[8,128]{1,0:T(8,128)S(1)}, u32[]{:S(2)}) copy-start(f32[8,128]{1,0:T(8,128)S(1)} %subtract_convert_fusion) | copy-start | bytes 12292
  2.1 16.3 %collective-permute-start.1 = (f32[5,8,128]{2,0,1:T(8,128)S(1)}, f32[5,8,128]{2,0,1:T(8,128)S(1)}, u32[]{:S(2)}, u32[]{:S(2)}) collective-permute-start(f32[5,8,128]{2,0,1:T(8,128)S(1)} %copy_multiply_fusion), channel_id=1, source_target_pairs={{1,0},{2,1},{3,2},{4,3},{5,4},{6,5},{7,6},{8,7},{9,8},{10,9},{11,1... | collective-permute-start | bytes 61448 | tf_op jit(solution)/shard_map/ppermute | solution.py:35
  4.7 13.7 %collective-permute-start = (f32[5,8,128]{2,0,1:T(8,128)S(1)}, f32[5,8,128]{2,0,1:T(8,128)S(1)}, u32[]{:S(2)}, u32[]{:S(2)}) collective-permute-start(f32[5,8,128]{2,0,1:T(8,128)S(1)} %copy_multiply_fusion), channel_id=1, source_target_pairs={{0,1},{1,2},{2,3},{3,4},{4,5},{5,6},{6,7},{7,8},{8,9},{9,10},{10,1... | collective-permute-start | bytes 61448 | tf_op jit(solution)/shard_map/ppermute | solution.py:32
  18.0 6.7 %copy-start.33 = (s32[16,2,128]{2,1,0:T(2,128)}, s32[16,2,128]{2,1,0:T(2,128)S(1)}, u32[]{:S(2)}) copy-start(s32[16,2,128]{2,1,0:T(2,128)S(1)} %eq.68) | copy-start | bytes 49156
  18.2 9.5 %copy-start.35 = (s32[16,2,128]{2,1,0:T(2,128)}, s32[16,2,128]{2,1,0:T(2,128)S(1)}, u32[]{:S(2)}) copy-start(s32[16,2,128]{2,1,0:T(2,128)S(1)} %eq.64) | copy-start | bytes 49156
  18.3 10.2 %copy-start.37 = (s32[16,2,128]{2,1,0:T(2,128)}, s32[16,2,128]{2,1,0:T(2,128)S(1)}, u32[]{:S(2)}) copy-start(s32[16,2,128]{2,1,0:T(2,128)S(1)} %eq.60) | copy-start | bytes 49156
  28.4 42.0 %copy-start.17 = (s32[16,256]{1,0:T(8,128)S(1)}, s32[16,256]{1,0:T(8,128)}, u32[]{:S(2)}) copy-start(s32[16,256]{1,0:T(8,128)} %param.24) | copy-start | bytes 49156
  30.9 54.9 %copy-start = (f32[60,16,256]{2,1,0:T(8,128)S(1)}, f32[60,16,256]{2,1,0:T(8,128)}, u32[]{:S(2)}) copy-start(f32[60,16,256]{2,1,0:T(8,128)} %param.23) | copy-start | bytes 2949124
  31.7 17.2 %collective-permute-start.3 = (f32[7,16,1]{2,1,0:T(8,128)S(1)}, f32[7,16,1]{2,1,0:T(8,128)S(1)}, u32[]{:S(2)}, u32[]{:S(2)}) collective-permute-start(f32[7,16,1]{2,1,0:T(8,128)S(1)} %get-tuple-element.104), channel_id=1, source_target_pairs={{32,0},{64,32},{96,64},{128,96},{160,128},{192,160},{224,192},{256... | collective-permute-start | bytes 1352 | tf_op jit(solution)/shard_map/ppermute | solution.py:35
  47.0 7.0 %collective-permute-start.2 = (f32[7,16,1]{2,1,0:T(8,128)S(1)}, f32[7,16,1]{2,1,0:T(8,128)S(1)}, u32[]{:S(2)}, u32[]{:S(2)}) collective-permute-start(f32[7,16,1]{2,1,0:T(8,128)S(1)} %get-tuple-element.103), channel_id=1, source_target_pairs={{0,32},{32,64},{64,96},{96,128},{128,160},{160,192},{192,224},{224... | collective-permute-start | bytes 1352 | tf_op jit(solution)/shard_map/ppermute | solution.py:32
  54.1 9.2 %collective-permute-start.5 = (f32[7,1,258]{2,1,0:T(1,128)S(1)}, f32[7,1,258]{2,1,0:T(1,128)S(1)}, u32[]{:S(2)}, u32[]{:S(2)}) collective-permute-start(f32[7,1,258]{2,1,0:T(1,128)S(1)} %get-tuple-element.98), channel_id=1, source_target_pairs={{1,0},{2,1},{3,2},{4,3},{5,4},{6,5},{7,6},{8,7},{9,8},{10,9},{11,1... | collective-permute-start | bytes 21680 | tf_op jit(solution)/shard_map/ppermute | solution.py:35
  56.1 8.1 %collective-permute-start.4 = (f32[7,1,258]{2,1,0:T(1,128)S(1)}, f32[7,1,258]{2,1,0:T(1,128)S(1)}, u32[]{:S(2)}, u32[]{:S(2)}) collective-permute-start(f32[7,1,258]{2,1,0:T(1,128)S(1)} %get-tuple-element.97), channel_id=1, source_target_pairs={{0,1},{1,2},{2,3},{3,4},{4,5},{5,6},{6,7},{7,8},{8,9},{9,10},{10,1... | collective-permute-start | bytes 21680 | tf_op jit(solution)/shard_map/ppermute | solution.py:32
  63.3 45.2 %copy-start.39 = (f32[18]{0:T(128)}, f32[18]{0:T(128)S(1)}, u32[]{:S(2)}) copy-start(f32[18]{0:T(128)S(1)} %or_select_fusion) | copy-start | bytes 220
  65.2 5.3 %collective-permute-start.7 = (f32[7,16,1]{2,1,0:T(8,128)S(1)}, f32[7,16,1]{2,1,0:T(8,128)S(1)}, u32[]{:S(2)}, u32[]{:S(2)}) collective-permute-start(f32[7,16,1]{2,1,0:T(8,128)S(1)} %get-tuple-element.102), channel_id=1, source_target_pairs={{32,0},{64,32},{96,64},{128,96},{160,128},{192,160},{224,192},{256... | collective-permute-start | bytes 1352 | tf_op jit(solution)/shard_map/ppermute | solution.py:35
  67.1 7.0 %collective-permute-start.6 = (f32[7,16,1]{2,1,0:T(8,128)S(1)}, f32[7,16,1]{2,1,0:T(8,128)S(1)}, u32[]{:S(2)}, u32[]{:S(2)}) collective-permute-start(f32[7,16,1]{2,1,0:T(8,128)S(1)} %get-tuple-element.101), channel_id=1, source_target_pairs={{0,32},{32,64},{64,96},{96,128},{128,160},{160,192},{192,224},{224... | collective-permute-start | bytes 1352 | tf_op jit(solution)/shard_map/ppermute | solution.py:32
  74.3 12.6 %collective-permute-start.9 = (f32[7,1,258]{2,1,0:T(1,128)S(1)}, f32[7,1,258]{2,1,0:T(1,128)S(1)}, u32[]{:S(2)}, u32[]{:S(2)}) collective-permute-start(f32[7,1,258]{2,1,0:T(1,128)S(1)} %get-tuple-element.96), channel_id=1, source_target_pairs={{1,0},{2,1},{3,2},{4,3},{5,4},{6,5},{7,6},{8,7},{9,8},{10,9},{11,1... | collective-permute-start | bytes 21680 | tf_op jit(solution)/shard_map/ppermute | solution.py:35
  76.2 10.7 %collective-permute-start.8 = (f32[7,1,258]{2,1,0:T(1,128)S(1)}, f32[7,1,258]{2,1,0:T(1,128)S(1)}, u32[]{:S(2)}, u32[]{:S(2)}) collective-permute-start(f32[7,1,258]{2,1,0:T(1,128)S(1)} %get-tuple-element.95), channel_id=1, source_target_pairs={{0,1},{1,2},{2,3},{3,4},{4,5},{5,6},{6,7},{7,8},{8,9},{9,10},{10,1... | collective-permute-start | bytes 21680 | tf_op jit(solution)/shard_map/ppermute | solution.py:32
  85.7 21.8 %copy-start.30 = (s32[4,16,2]{1,2,0:T(2,128)S(1)}, s32[4,16,2]{1,2,0:T(2,128)}, u32[]{:S(2)}) copy-start(s32[4,16,2]{1,2,0:T(2,128)} %param.27) | copy-start | bytes 1540
  87.9 5.3 %collective-permute-start.11 = (f32[7,16,1]{2,1,0:T(8,128)S(1)}, f32[7,16,1]{2,1,0:T(8,128)S(1)}, u32[]{:S(2)}, u32[]{:S(2)}) collective-permute-start(f32[7,16,1]{2,1,0:T(8,128)S(1)} %get-tuple-element.100), channel_id=1, source_target_pairs={{32,0},{64,32},{96,64},{128,96},{160,128},{192,160},{224,192},{256... | collective-permute-start | bytes 1352 | tf_op jit(solution)/shard_map/ppermute | solution.py:35
  89.8 7.0 %collective-permute-start.10 = (f32[7,16,1]{2,1,0:T(8,128)S(1)}, f32[7,16,1]{2,1,0:T(8,128)S(1)}, u32[]{:S(2)}, u32[]{:S(2)}) collective-permute-start(f32[7,16,1]{2,1,0:T(8,128)S(1)} %get-tuple-element.99), channel_id=1, source_target_pairs={{0,32},{32,64},{64,96},{96,128},{128,160},{160,192},{192,224},{224... | collective-permute-start | bytes 1352 | tf_op jit(solution)/shard_map/ppermute | solution.py:32
  97.0 11.2 %collective-permute-start.13 = (f32[7,1,258]{2,1,0:T(1,128)S(1)}, f32[7,1,258]{2,1,0:T(1,128)S(1)}, u32[]{:S(2)}, u32[]{:S(2)}) collective-permute-start(f32[7,1,258]{2,1,0:T(1,128)S(1)} %get-tuple-element.94), channel_id=1, source_target_pairs={{1,0},{2,1},{3,2},{4,3},{5,4},{6,5},{7,6},{8,7},{9,8},{10,9},{11,1... | collective-permute-start | bytes 21680 | tf_op jit(solution)/shard_map/ppermute | solution.py:35
  98.9 9.4 %collective-permute-start.12 = (f32[7,1,258]{2,1,0:T(1,128)S(1)}, f32[7,1,258]{2,1,0:T(1,128)S(1)}, u32[]{:S(2)}, u32[]{:S(2)}) collective-permute-start(f32[7,1,258]{2,1,0:T(1,128)S(1)} %get-tuple-element.93), channel_id=1, source_target_pairs={{0,1},{1,2},{2,3},{3,4},{4,5},{5,6},{6,7},{7,8},{8,9},{9,10},{10,1... | collective-permute-start | bytes 21680 | tf_op jit(solution)/shard_map/ppermute | solution.py:32
  109.0 26.4 %copy-start.20 = (f32[16,256]{1,0:T(8,128)}, f32[16,256]{1,0:T(8,128)S(1)}, u32[]{:S(2)}) copy-start(f32[16,256]{1,0:T(8,128)S(1)} %get-tuple-element.56) | copy-start | bytes 49156
  109.0 63.8 %copy-start.8 = (f32[16,256]{1,0:T(8,128)}, f32[16,256]{1,0:T(8,128)S(1)}, u32[]{:S(2)}) copy-start(f32[16,256]{1,0:T(8,128)S(1)} %get-tuple-element.57) | copy-start | bytes 49156
  109.0 63.8 %copy-start.9 = (f32[16,256]{1,0:T(8,128)}, f32[16,256]{1,0:T(8,128)S(1)}, u32[]{:S(2)}) copy-start(f32[16,256]{1,0:T(8,128)S(1)} %get-tuple-element.58) | copy-start | bytes 49156
  109.3 9.8 %collective-permute-start.15 = (f32[63,16,1]{2,1,0:T(8,128)S(1)}, f32[63,16,1]{2,1,0:T(8,128)S(1)}, u32[]{:S(2)}, u32[]{:S(2)}) collective-permute-start(f32[63,16,1]{2,1,0:T(8,128)S(1)} %get-tuple-element.72), channel_id=1, source_target_pairs={{32,0},{64,32},{96,64},{128,96},{160,128},{192,160},{224,192},{256... | collective-permute-start | bytes 12104 | tf_op jit(solution)/shard_map/ppermute | solution.py:35
  111.3 11.9 %collective-permute-start.14 = (f32[63,16,1]{2,1,0:T(8,128)S(1)}, f32[63,16,1]{2,1,0:T(8,128)S(1)}, u32[]{:S(2)}, u32[]{:S(2)}) collective-permute-start(f32[63,16,1]{2,1,0:T(8,128)S(1)} %get-tuple-element.71), channel_id=1, source_target_pairs={{0,32},{32,64},{64,96},{96,128},{128,160},{160,192},{192,224},{224... | collective-permute-start | bytes 12104 | tf_op jit(solution)/shard_map/ppermute | solution.py:32
  123.8 12.2 %collective-permute-start.17 = (f32[63,1,258]{2,1,0:T(1,128)S(1)}, f32[63,1,258]{2,1,0:T(1,128)S(1)}, u32[]{:S(2)}, u32[]{:S(2)}) collective-permute-start(f32[63,1,258]{2,1,0:T(1,128)S(1)} %get-tuple-element.68), channel_id=1, source_target_pairs={{1,0},{2,1},{3,2},{4,3},{5,4},{6,5},{7,6},{8,7},{9,8},{10,9},{11,1... | collective-permute-start | bytes 195056 | tf_op jit(solution)/shard_map/ppermute | solution.py:35
  125.7 10.6 %collective-permute-start.16 = (f32[63,1,258]{2,1,0:T(1,128)S(1)}, f32[63,1,258]{2,1,0:T(1,128)S(1)}, u32[]{:S(2)}, u32[]{:S(2)}) collective-permute-start(f32[63,1,258]{2,1,0:T(1,128)S(1)} %get-tuple-element.67), channel_id=1, source_target_pairs={{0,1},{1,2},{2,3},{3,4},{4,5},{5,6},{6,7},{7,8},{8,9},{9,10},{10,1... | collective-permute-start | bytes 195056 | tf_op jit(solution)/shard_map/ppermute | solution.py:32
  137.4 14.6 %copy-start.13 = (f32[17,258]{1,0:T(8,128)}, f32[17,258]{1,0:T(8,128)S(1)}, u32[]{:S(2)}) copy-start(f32[17,258]{1,0:T(8,128)S(1)} %fusion.72) | copy-start | bytes 52636
  145.5 6.4 %copy-start.7 = (f32[63,1,258]{2,1,0:T(1,128)S(1)}, f32[63,1,258]{2,1,0:T(1,128)}, u32[]{:S(2)}) copy-start(f32[63,1,258]{2,1,0:T(1,128)} %copy-done.6) | copy-start | bytes 195052
  146.4 5.6 %copy-start.12 = (f32[63,1,258]{2,1,0:T(1,128)S(1)}, f32[63,1,258]{2,1,0:T(1,128)}, u32[]{:S(2)}) copy-start(f32[63,1,258]{2,1,0:T(1,128)} %copy-done.11) | copy-start | bytes 195052
  146.6 12.4 %collective-permute-start.19 = (f32[60,16,1]{2,1,0:T(8,128)S(1)}, f32[60,16,1]{2,1,0:T(8,128)S(1)}, u32[]{:S(2)}, u32[]{:S(2)}) collective-permute-start(f32[60,16,1]{2,1,0:T(8,128)S(1)} %get-tuple-element.74), channel_id=1, source_target_pairs={{32,0},{64,32},{96,64},{128,96},{160,128},{192,160},{224,192},{256... | collective-permute-start | bytes 11528 | tf_op jit(solution)/shard_map/ppermute | solution.py:35
  148.6 11.7 %collective-permute-start.18 = (f32[60,16,1]{2,1,0:T(8,128)S(1)}, f32[60,16,1]{2,1,0:T(8,128)S(1)}, u32[]{:S(2)}, u32[]{:S(2)}) collective-permute-start(f32[60,16,1]{2,1,0:T(8,128)S(1)} %get-tuple-element.73), channel_id=1, source_target_pairs={{0,32},{32,64},{64,96},{96,128},{128,160},{160,192},{192,224},{224... | collective-permute-start | bytes 11528 | tf_op jit(solution)/shard_map/ppermute | solution.py:32
  161.6 11.4 %collective-permute-start.21 = (f32[60,1,258]{2,1,0:T(1,128)S(1)}, f32[60,1,258]{2,1,0:T(1,128)S(1)}, u32[]{:S(2)}, u32[]{:S(2)}) collective-permute-start(f32[60,1,258]{2,1,0:T(1,128)S(1)} %get-tuple-element.70), channel_id=1, source_target_pairs={{1,0},{2,1},{3,2},{4,3},{5,4},{6,5},{7,6},{8,7},{9,8},{10,9},{11,1... | collective-permute-start | bytes 185768 | tf_op jit(solution)/shard_map/ppermute | solution.py:35
  163.6 10.6 %collective-permute-start.20 = (f32[60,1,258]{2,1,0:T(1,128)S(1)}, f32[60,1,258]{2,1,0:T(1,128)S(1)}, u32[]{:S(2)}, u32[]{:S(2)}) collective-permute-start(f32[60,1,258]{2,1,0:T(1,128)S(1)} %get-tuple-element.69), channel_id=1, source_target_pairs={{0,1},{1,2},{2,3},{3,4},{4,5},{5,6},{6,7},{7,8},{8,9},{9,10},{10,1... | collective-permute-start | bytes 185768 | tf_op jit(solution)/shard_map/ppermute | solution.py:32
  179.3 4.1 %copy-start.36 = (s32[16,2,128]{2,1,0:T(2,128)S(1)}, s32[16,2,128]{2,1,0:T(2,128)}, u32[]{:S(2)}) copy-start(s32[16,2,128]{2,1,0:T(2,128)} %copy-done.35) | copy-start | bytes 49156
  181.2 7.7 %copy-start.10 = (f32[60,16,256]{2,1,0:T(8,128)}, f32[60,16,256]{2,1,0:T(8,128)S(1)}, u32[]{:S(2)}) copy-start(f32[60,16,256]{2,1,0:T(8,128)S(1)} %fusion.31) | copy-start | bytes 2949124
  181.3 5.9 %copy-start.32 = (s32[16,2,128]{2,1,0:T(2,128)S(1)}, s32[16,2,128]{2,1,0:T(2,128)}, u32[]{:S(2)}) copy-start(s32[16,2,128]{2,1,0:T(2,128)} %copy-done.31) | copy-start | bytes 49156
  181.4 7.6 %copy-start.44 = (s32[16,2]{0,1:T(2,128)S(1)}, s32[16,2]{0,1:T(2,128)}, u32[]{:S(2)}) copy-start(s32[16,2]{0,1:T(2,128)} %get-tuple-element.132) | copy-start | bytes 388
  181.4 7.9 %copy-start.43 = (s32[16,2]{0,1:T(2,128)S(1)}, s32[16,2]{0,1:T(2,128)}, u32[]{:S(2)}) copy-start(s32[16,2]{0,1:T(2,128)} %get-tuple-element.131) | copy-start | bytes 388
  181.6 8.0 %copy-start.42 = (s32[16,2]{0,1:T(2,128)S(1)}, s32[16,2]{0,1:T(2,128)}, u32[]{:S(2)}) copy-start(s32[16,2]{0,1:T(2,128)} %get-tuple-element.133) | copy-start | bytes 388
  181.6 8.3 %copy-start.41 = (s32[16,2]{0,1:T(2,128)S(1)}, s32[16,2]{0,1:T(2,128)}, u32[]{:S(2)}) copy-start(s32[16,2]{0,1:T(2,128)} %get-tuple-element.130) | copy-start | bytes 388
  181.6 34.4 %copy-start.29 = (f32[8,128]{1,0:T(8,128)S(1)}, f32[8,128]{1,0:T(8,128)}, u32[]{:S(2)}) copy-start(f32[8,128]{1,0:T(8,128)} %copy-done.28) | copy-start | bytes 12292
  190.2 19.1 %collective-permute-start.25 = (f32[8,128]{1,0:T(8,128)S(1)}, f32[8,128]{1,0:T(8,128)S(1)}, u32[]{:S(2)}, u32[]{:S(2)}) collective-permute-start(f32[8,128]{1,0:T(8,128)S(1)} %get-tuple-element.125), channel_id=1, source_target_pairs={{0,1},{1,2},{2,3},{3,4},{4,5},{5,6},{6,7},{7,8},{8,9},{9,10},{10,1... | collective-permute-start | bytes 12296 | tf_op jit(solution)/shard_map/ppermute | solution.py:43
  198.2 11.1 %collective-permute-start.24 = (f32[8,128]{1,0:T(8,128)S(1)}, f32[8,128]{1,0:T(8,128)S(1)}, u32[]{:S(2)}, u32[]{:S(2)}) collective-permute-start(f32[8,128]{1,0:T(8,128)S(1)} %get-tuple-element.124), channel_id=1, source_target_pairs={{1,0},{2,1},{3,2},{4,3},{5,4},{6,5},{7,6},{8,7},{9,8},{10,9},{11,1... | collective-permute-start | bytes 12296 | tf_op jit(solution)/shard_map/ppermute | solution.py:43
  200.1 9.2 %collective-permute-start.23 = (f32[4,8,128]{2,1,0:T(8,128)S(1)}, f32[4,8,128]{2,1,0:T(8,128)S(1)}, u32[]{:S(2)}, u32[]{:S(2)}) collective-permute-start(f32[4,8,128]{2,1,0:T(8,128)S(1)} %get-tuple-element.127), channel_id=1, source_target_pairs={{0,1},{1,2},{2,3},{3,4},{4,5},{5,6},{6,7},{7,8},{8,9},{9,10},{10,1... | collective-permute-start | bytes 49160 | tf_op jit(solution)/shard_map/ppermute | solution.py:43
  207.4 8.7 %collective-permute-start.22 = (f32[4,8,128]{2,1,0:T(8,128)S(1)}, f32[4,8,128]{2,1,0:T(8,128)S(1)}, u32[]{:S(2)}, u32[]{:S(2)}) collective-permute-start(f32[4,8,128]{2,1,0:T(8,128)S(1)} %get-tuple-element.126), channel_id=1, source_target_pairs={{1,0},{2,1},{3,2},{4,3},{5,4},{6,5},{7,6},{8,7},{9,8},{10,9},{11,1... | collective-permute-start | bytes 49160 | tf_op jit(solution)/shard_map/ppermute | solution.py:43
  (25 other events, 52.8 us)
where the time goes:
time: 218 us; the launch traced here: 217 us
  starting transfers between devices  120 us (55%)
  other arithmetic  33.6 us (15%)
  waiting for transfers between devices  27.1 us (12%)
  matrix products  18.1 us (8%)
  local copies, waits for them, and re-layouts  16.1 us (7%)
    ppermute x11, starting transfers between devices, padded_2(): lax.ppermute(lax.slice_in_dim(block, block.shape[dim] - width, None, axis...  65.8 us
    ppermute x11, starting transfers between devices, padded_2(): lax.ppermute(lax.slice_in_dim(block, 0, width, axis=dim), axis, backward)  35.1 us
    ppermute x11, waiting for transfers between devices, padded_2(): lax.ppermute(lax.slice_in_dim(block, block.shape[dim] - width, None, axis...  20 us
    ppermute x4, starting transfers between devices, shifted(): return lax.ppermute(array, axis, pairs)  19 us
    dot_general x4, matrix products, regrid_forward(): jnp.einsum('rbjc,frbc->frbj', onehot, picked, precision=lax.Precision.HIG...  9.61 us
    dot_general x4, matrix products, regrid_back(): jnp.einsum('rbjc,srbj->srbc', onehot, shares, precision=lax.Precision.HIG...  7.33 us
    mul x2, other arithmetic, laplace(): flux_north = north_open * (field[..., 1:, :] - field[..., :-1, :])  7.28 us
    mul x1, other arithmetic, horizontal_tendency(): north_open * speed_north * 0.5  6.97 us
  transfers between devices with their start and end apart: 26, of which 11 were waited for; matrix products, arithmetic and copies ran while one was open for 10% of the time, Pallas kernels for 0%

commit v1 on v0

v1 whole, which is shorter than its diff:
```python
import math

import jax
import jax.numpy as jnp
from jax import lax
from jax.experimental import pallas as pl
from jax.experimental.pallas import tpu as pltpu
from jax.sharding import PartitionSpec as P

SUBS = 3
grav_step = 0.6
height_step = 0.6
wind_step = 0.5
fresh_step = 0.5
mixing_fourth = 0.02
advect_coef = 0.1
diapycnal_diffusion = 0.2
heat_gain = 0.3
light_gain = 0.3
light_decay = 8.0
depth_floor = 0.25
area_floor = 1.0

f32 = jnp.float32
bf16 = jnp.bfloat16

FLUX_ORDER = (0, 1, 4, 2, 3)


def lanes(shape):
    return lax.broadcasted_iota(jnp.int32, shape, len(shape) - 1)


def subs(shape):
    return lax.broadcasted_iota(jnp.int32, shape, len(shape) - 2)


def roll(x, shift, axis):
    return pltpu.roll(x, shift % x.shape[axis], axis)


def east(x):
    return roll(x, -1, 1)


def west(x):
    return roll(x, 1, 1)


def north(x):
    return roll(x, -1, 0)


def south(x):
    return roll(x, 1, 0)


def put(ref, value):
    for b in range(3):
        ref[b] = value[:, b * 128:b * 128 + 128]


def whole(ref):
    return jnp.concatenate([ref[b] for b in range(3)], axis=1)


def own_part(ref):
    return jnp.concatenate([ref[b, 0:16] for b in range(2)], axis=1)


def kernel(
    h_in, u_in, v_in, t_in, n_in, x_in, flag_in, tile, pt_in, w_in,
    o_height, o_zonal, o_meridional, tnew, o_skin,
    planes, count_int, tn, flux, flags, pt, wt,
    rows_in, rows_wide, masked, rx, col_e, col_w, rcol_e, rcol_w, rdiag, rns,
    tv, tpack, rt_e, rt_w, rt_diag,
    forcing, fcol_e, fcol_w, rf_e, rf_w, rf_diag, rf_ns,
    cnt_r, me_r, mn_r, se_r, sn_r,
    lap, mix, tpart, flow, rowcol, row_hot, sv, cells, table, rtable, top_part,
    in_sem, send_sem, recv_sem,
):
    strata = t_in.shape[0] // 16
    n_lon, n_lat = lax.axis_size("lon"), lax.axis_size("lat")
    lon, lat = lax.axis_index("lon"), lax.axis_index("lat")
    le, lw = lax.rem(lon + 1, n_lon), lax.rem(lon + n_lon - 1, n_lon)
    ln, ls = lax.rem(lat + 1, n_lat), lax.rem(lat + n_lat - 1, n_lat)
    to_n, to_s = {"lon": lon, "lat": ln}, {"lon": lon, "lat": ls}
    to_e, to_w = {"lon": le, "lat": lat}, {"lon": lw, "lat": lat}
    to_ne, to_nw = {"lon": le, "lat": ln}, {"lon": lw, "lat": ln}
    to_se, to_sw = {"lon": le, "lat": ls}, {"lon": lw, "lat": ls}

    loads = [
        (x_in, flux), (flag_in, flags), (n_in, count_int), (h_in, planes.at[0]), (u_in, planes.at[1]),
        (v_in, planes.at[2]), (t_in.at[pl.ds(0, 16)], planes.at[4]),
        (pt_in.at[:, pl.ds(0, 128)], pt.at[0]), (pt_in.at[:, pl.ds(128, 128)], pt.at[1]),
        (w_in.at[:, pl.ds(0, 128)], wt.at[0]), (w_in.at[:, pl.ds(128, 128)], wt.at[1]),
        (tile, rows_in), (t_in.at[:, pl.ds(0, 128)], tn.at[0, pl.ds(0, strata * 16)]),
        (t_in.at[:, pl.ds(128, 128)], tn.at[1, pl.ds(0, strata * 16)]),
    ]
    load = [pltpu.make_async_copy(a, b, in_sem.at[i]) for i, (a, b) in enumerate(loads)]
    for c in load:
        c.start()

    barrier = pltpu.get_barrier_semaphore()
    for where in (to_n, to_s, to_e, to_w, to_ne, to_nw, to_se, to_sw):
        pl.semaphore_signal(barrier, inc=1, device_id=where, device_id_type=pl.DeviceIdType.MESH)

    sends = []

    def send(src, dst, where):
        i = len(sends)
        c = pltpu.make_async_remote_copy(
            src_ref=src, dst_ref=dst, send_sem=send_sem.at[i], recv_sem=recv_sem.at[i],
            device_id=where, device_id_type=pl.DeviceIdType.MESH,
        )
        c.start()
        sends.append(c)
        return c

    lane = lanes((8, 128))
    sub = subs((8, 128))

    load[0].wait()
    load[1].wait()
    open_sea = (1 - flags[...]).astype(f32)
    for f, g in enumerate(FLUX_ORDER):
        masked[f * 8:f * 8 + 8] = flux[g * 8:g * 8 + 8] * open_sea
    for i in range(2, 7):
        load[i].wait()
    planes[3] = count_int[...].astype(f32)

    def pack_columns(tiles, n, dst_e, dst_w):
        for rt in range(2):
            pe = pw = jnp.zeros((8, 128), f32)
            for p in range(n):
                here = (lane >= 3 * p) & (lane < 3 * p + 3)
                pe = jnp.where(here, roll(tiles(p, rt, 1), 3 * p - 125, 1), pe)
                pw = jnp.where(here, roll(tiles(p, rt, 0), 3 * p, 1), pw)
            dst_e[rt * 8:rt * 8 + 8] = pe
            dst_w[rt * 8:rt * 8 + 8] = pw

    def plane_tile(p, rt, b):
        return planes[p, rt * 8:rt * 8 + 8, b * 128:b * 128 + 128]

    pack_columns(plane_tile, 5, col_e, col_w)

    pl.semaphore_wait(barrier, 8)

    x_n = send(masked, rx.at[0], to_n)
    x_s = send(masked, rx.at[1], to_s)
    p_copies = [
        send(col_e, rcol_w, to_e),
        send(col_w, rcol_e, to_w),
        send(col_e.at[pl.ds(8, 8)], rdiag.at[3], to_ne),
        send(col_w.at[pl.ds(8, 8)], rdiag.at[2], to_nw),
        send(col_e.at[pl.ds(0, 8)], rdiag.at[1], to_se),
        send(col_w.at[pl.ds(0, 8)], rdiag.at[0], to_sw),
        send(planes.at[:, pl.ds(8, 8)], rns.at[1], to_n),
        send(planes.at[:, pl.ds(0, 8)], rns.at[0], to_s),
    ]

    load[11].wait()
    for j in range(8):
        rows_wide[j:j + 1, 0:16] = rows_in[j // 2, j % 2:j % 2 + 1, :].astype(f32)
    row_of = jnp.zeros((8, 128), f32)
    for j in range(8):
        here = lax.shift_right_logical(lane, 4) == j
        row_of = jnp.where(here, roll(jnp.broadcast_to(rows_wide[j:j + 1, :], (8, 128)), 16 * j, 1), row_of)
    row_id = subs((128, 128))
    hot = (row_id & 31).astype(f32) == jnp.concatenate([row_of] * 16, axis=0)
    hot = jnp.where(hot & (row_id < 96), 1.0, 0.0)
    row_hot[...] = hot[0:32].astype(bf16)
    rowcol[...] = jnp.transpose(hot).astype(bf16)

    load[12].wait()
    load[13].wait()
    pad = 64 * 16 - strata * 16
    for b in range(2):
        tn[b, strata * 16:] = jnp.zeros((pad, 128), f32)

    half = lax.shift_right_logical(lane, 1)

    def turn(r, carry):
        carry = list(carry)
        for q in range(8):
            g, q4 = q // 4, q % 4
            here = half == r + 16 * q4
            t0 = tn[0, pl.ds(q * 128 + r, 8, stride=16), :]
            t1 = tn[1, pl.ds(q * 128 + r, 8, stride=16), :]
            tv[r, q * 8:q * 8 + 8, 0:128] = t0
            tv[r, q * 8:q * 8 + 8, 128:256] = t1
            at = 2 * r + 32 * q4
            carry[g] = jnp.where(here, pltpu.roll(t1, lax.rem(at + 2, 128), 1), carry[g])
            carry[2 + g] = jnp.where(here, pltpu.roll(t0, at, 1), carry[2 + g])
        return tuple(carry)

    packs = lax.fori_loop(0, 16, turn, (jnp.zeros((8, 128), f32),) * 4, unroll=4)
    for i in range(4):
        tpack[i // 2, (i % 2) * 8:(i % 2) * 8 + 8] = packs[i]

    t_copies = [
        send(tpack.at[0], rt_w, to_e),
        send(tpack.at[1], rt_e, to_w),
        send(tpack.at[0], rt_diag.at[3], to_ne),
        send(tpack.at[1], rt_diag.at[2], to_nw),
        send(tpack.at[0], rt_diag.at[1], to_se),
        send(tpack.at[1], rt_diag.at[0], to_sw),
        send(tv.at[pl.ds(14, 2), :, pl.ds(0, 256)], tv.at[pl.ds(22, 2), :, pl.ds(0, 256)], to_n),
        send(tv.at[pl.ds(0, 2), :, pl.ds(0, 256)], tv.at[pl.ds(16, 2), :, pl.ds(0, 256)], to_s),
    ]

    for i in range(7, 11):
        load[i].wait()

    x_n.wait_recv()
    x_s.wait_recv()
    keep_south = jnp.broadcast_to(lat, (8, 128)) > 0
    keep_north = jnp.broadcast_to(lat, (8, 128)) < n_lat - 1
    zero = jnp.zeros((8, 128), f32)
    for f in range(5):
        part = slice(f * 8, f * 8 + 8)
        bands = jnp.concatenate(
            [jnp.where(keep_south, rx[0, part], 0.0), masked[part], jnp.where(keep_north, rx[1, part], 0.0), zero], axis=0
        )
        high = bands.astype(bf16)
        rest = bands - high.astype(f32)
        mid = rest.astype(bf16)
        low = (rest - mid.astype(f32)).astype(bf16)
        picked = jnp.dot(
            rowcol[...], jnp.concatenate([high, mid, low, jnp.zeros((32, 128), bf16)], axis=0), preferred_element_type=f32
        )
        for b in range(2):
            for rt in range(2):
                acc = zero
                for k in range(4):
                    m = (k * 2 + b) * 16 + rt * 8
                    at = slice(k * 16 + rt * 8, k * 16 + rt * 8 + 8)
                    cell = jnp.take_along_axis(picked[m:m + 8], pt[b, at], axis=1, mode="promise_in_bounds")
                    acc = acc + cell * wt[b, at]
                forcing[b, rt * 64 + f * 8:rt * 64 + f * 8 + 8] = acc

    def forcing_tile(f, rt, b):
        return forcing[b, rt * 64 + f * 8:rt * 64 + f * 8 + 8]

    pack_columns(forcing_tile, 3, fcol_e, fcol_w)

    f_copies = [
        send(fcol_e, rf_w, to_e),
        send(fcol_w, rf_e, to_w),
        send(fcol_e.at[pl.ds(8, 8)], rf_diag.at[3], to_ne),
        send(fcol_w.at[pl.ds(8, 8)], rf_diag.at[2], to_nw),
        send(fcol_e.at[pl.ds(0, 8)], rf_diag.at[1], to_se),
        send(fcol_w.at[pl.ds(0, 8)], rf_diag.at[0], to_sw),
        send(forcing.at[:, pl.ds(64, 24)], rf_ns.at[1], to_n),
        send(forcing.at[:, pl.ds(0, 24)], rf_ns.at[0], to_s),
    ]

    def extended(p, tiles, ns, ce, cw, diag):
        def side(e, w):
            return jnp.where(lane < 64, roll(e, -3 * p, 1), roll(w, 125 - 3 * p, 1))

        rows = []
        for rt in range(2):
            part = slice(rt * 8, rt * 8 + 8)
            rows.append(jnp.concatenate([tiles(p, rt, 0), tiles(p, rt, 1), side(ce[part], cw[part])], axis=1))
        edge = [jnp.where(sub < 4, ns(0, p, b), ns(1, p, b)) for b in range(2)]
        corner = jnp.where(sub < 4, side(diag[0], diag[1]), side(diag[2], diag[3]))
        rows.append(jnp.concatenate(edge + [corner], axis=1))
        return jnp.concatenate(rows, axis=0)

    for c in p_copies:
        c.wait_recv()

    def plane_ns(i, p, b):
        return rns[i, p, :, b * 128:b * 128 + 128]

    height, zonal, meridional, count, top = [
        extended(p, plane_tile, plane_ns, rcol_e, rcol_w, rdiag) for p in range(5)
    ]
    row_ids = subs((24, 384))
    off_grid = ((lat == n_lat - 1) & (row_ids >= 16) & (row_ids < 20)) | ((lat == 0) & (row_ids >= 20))
    count = jnp.where(off_grid, 0.0, count)

    scale = 1.0 / (2.0 * strata)

    def depth(c):
        return c * scale + c * (c - 1.0) * (scale / strata)

    min_e = jnp.minimum(count, east(count))
    min_n = jnp.minimum(count, north(count))
    put(cnt_r, count)
    put(me_r, min_e)
    put(mn_r, min_n)

    def plane_laplace(field):
        fe = jnp.where(whole(me_r) > 0.5, east(field) - field, 0.0)
        fn = jnp.where(whole(mn_r) > 0.5, north(field) - field, 0.0)
        return fe - west(fe) + fn - south(fn)

    wet_own = (own_part(cnt_r) > 0.5).astype(f32)
    top_mix = plane_laplace(plane_laplace(top))[0:16, 0:256]

    def own_forcing(f):
        return jnp.concatenate(
            [jnp.concatenate([forcing_tile(f, rt, 0), forcing_tile(f, rt, 1)], axis=1) for rt in range(2)], axis=0
        )

    heat, light = own_forcing(3), own_forcing(4)
    absorb = 1.0 - math.exp(-1.0 / light_decay)
    t_own = planes[4]
    t_next = jnp.concatenate([tn[0, 16:32], tn[1, 16:32]], axis=1)
    top_part[...] = (
        t_own
        + wet_own
        * (
            diapycnal_diffusion * jnp.where(own_part(cnt_r) > 1.5, t_next - t_own, 0.0)
            + light_gain * absorb * light
            + heat_gain * heat
        )
        - mixing_fourth * top_mix
    )

    for c in t_copies:
        c.wait_recv()

    def unpack(r, _):
        for q in range(8):
            g, q4 = q // 4, q % 4
            at = 2 * r + 32 * q4
            e = pltpu.roll(rt_e[g * 8:g * 8 + 8], lax.rem(256 - at, 128), 1)
            w = pltpu.roll(rt_w[g * 8:g * 8 + 8], lax.rem(254 - at, 128), 1)
            tv[r, q * 8:q * 8 + 8, 256:384] = jnp.where(lane < 64, e, w)
        return 0

    lax.fori_loop(0, 16, unpack, 0, unroll=4)
    for row, r, i in ((16, 0, 0), (23, 15, 2)):
        for q in range(8):
            g, q4 = q // 4, q % 4
            at = 2 * r + 32 * q4
            e = roll(rt_diag[i, g * 8:g * 8 + 8], -at, 1)
            w = roll(rt_diag[i + 1, g * 8:g * 8 + 8], 126 - at, 1)
            tv[row, q * 8:q * 8 + 8, 256:384] = jnp.where(lane < 64, e, w)

    level = subs((8, 384)).astype(f32)

    def wide_row(ref, r):
        return jnp.concatenate([jnp.broadcast_to(ref[b, pl.ds(r, 1), :], (8, 128)) for b in range(3)], axis=1)

    me = wide_row(mn_r, 22)
    for q in range(8):
        part = slice(q * 8, q * 8 + 8)
        flow[part] = jnp.where(level + float(q * 8) < me, tv[23, part] - tv[22, part], 0.0)

    def lap_row(i, _):
        r, rn = lax.rem(i + 23, 24), lax.rem(i, 24)
        me, mn = wide_row(me_r, r), wide_row(mn_r, r)
        for q in range(8):
            part = slice(q * 8, q * 8 + 8)
            lev = level + float(q * 8)
            t = tv[r, part]
            fe = jnp.where(lev < me, east(t) - t, 0.0)
            fn = jnp.where(lev < mn, tv[rn, part] - t, 0.0)
            lap[r, part] = fe - west(fe) + fn - flow[part]
            flow[part] = fn
        return 0

    lax.fori_loop(0, 18, lap_row, 0)

    two = (slice(None), slice(0, 256))
    mn = wide_row(mn_r, 23)[two]
    for q in range(8):
        part = slice(q * 8, q * 8 + 8)
        rise = lap[0, part, 0:256] - lap[23, part, 0:256]
        flow[part, 0:256] = jnp.where(level[two] + float(q * 8) < mn, rise, 0.0)

    def mix_row(r, _):
        me, mn = wide_row(me_r, r), wide_row(mn_r, r)[two]
        for q in range(8):
            part = slice(q * 8, q * 8 + 8)
            lev = level + float(q * 8)
            t = lap[r, part]
            fe = jnp.where(lev < me, east(t) - t, 0.0)
            fn = jnp.where(lev[two] < mn, lap[r + 1, part, 0:256] - t[two], 0.0)
            mix[r, part] = (-mixing_fourth) * ((fe - west(fe))[two] + fn - flow[part, 0:256])
            flow[part, 0:256] = fn
        return 0

    lax.fori_loop(0, 16, mix_row, 0)

    for c in f_copies:
        c.wait_recv()

    def forcing_ns(i, f, b):
        return rf_ns[i, b, f * 8:f * 8 + 8]

    wind_e, wind_n, fresh = [
        extended(f, forcing_tile, forcing_ns, rf_e, rf_w, rf_diag) for f in range(3)
    ]
    min_e, min_n = whole(me_r), whole(mn_r)
    depth_e, depth_n = depth(min_e), depth(min_n)
    pull_e, pull_n = grav_step * depth_e, grav_step * depth_n
    push_e = jnp.where(min_e > 0.5, wind_step * wind_e, 0.0)
    push_n = jnp.where(min_n > 0.5, wind_step * wind_n, 0.0)
    gain = jnp.where(whole(cnt_r) > 0.5, fresh_step * fresh, 0.0)
    zonal = jnp.where(min_e > 0.5, zonal, 0.0)
    meridional = jnp.where(min_n > 0.5, meridional, 0.0)
    for _ in range(SUBS):
        zonal = zonal - pull_e * (east(height) - height) + push_e
        meridional = meridional - pull_n * (north(height) - height) + push_n
        height = height + gain - height_step * (zonal - west(zonal) + meridional - south(meridional))

    own = (slice(0, 16), slice(0, 256))
    o_height[...] = height[own]
    o_zonal[...] = zonal[own]
    o_meridional[...] = meridional[own]
    speed_e = zonal * ((-0.5 * advect_coef) / jnp.maximum(depth_e, depth_floor))
    speed_n = meridional * ((-0.5 * advect_coef) / jnp.maximum(depth_n, depth_floor))
    put(se_r, speed_e)
    put(sn_r, speed_n)

    ce = speed_e * (top + east(top))
    cn = speed_n * (top + north(top))
    top_new = top_part[...] + (ce - west(ce) + cn - south(cn))[own]
    inverse = wet_own / jnp.maximum(depth(own_part(cnt_r)), depth_floor)
    surface = [top_new * wet_own, height[own] * wet_own, zonal[own] * inverse, meridional[own] * inverse, wet_own]
    for s in range(8):
        for b in range(2):
            piece = surface[s][:, b * 128:b * 128 + 128] if s < 5 else jnp.zeros((16, 128), f32)
            sv[pl.ds(b * 8 + s, 16, stride=16), :] = piece

    cell_id = lax.broadcasted_iota(jnp.int32, (128, 128), 0).astype(f32).astype(bf16)

    def spread(r, _):
        for b in range(2):
            value = sv[pl.ds(pl.multiple_of(r * 16 + b * 8, 8), 8), :]
            for k in range(4):
                share = value * wt[b, pl.ds(k * 16 + r, 1), :]
                high = share.astype(bf16)
                low = (share - high.astype(f32)).astype(bf16)
                point = pt[b, pl.ds(k * 16 + r, 1), :].astype(f32).astype(bf16)
                by_cell = lax.dot_general(
                    jnp.concatenate([high, low], axis=0), jnp.where(cell_id == point, bf16(1), bf16(0)),
                    (((1,), (1,)), ((), ())), preferred_element_type=f32,
                )
                cells[pl.ds((k * 2 + b) * 16 + r, 8, stride=128), :] = by_cell[0:8] + by_cell[8:16]
        return 0

    lax.fori_loop(0, 16, spread, 0, unroll=2)

    for s in range(5):
        part = cells[s * 128:s * 128 + 128]
        high = part.astype(bf16)
        low = (part - high.astype(f32)).astype(bf16)
        rows = jnp.dot(row_hot[...], high, preferred_element_type=f32) + jnp.dot(
            row_hot[...], low, preferred_element_type=f32
        )
        for band in range(3):
            table[band, s * 8:s * 8 + 8] = rows[band * 8:band * 8 + 8]

    s_s = send(table.at[0], rtable.at[1], to_s)
    s_n = send(table.at[2], rtable.at[0], to_n)

    def vertical(i, carry):
        fade, below = carry
        below = list(below)
        for j in range(4):
            l = i * 4 + j
            lev = (l + 0).astype(f32)
            for rt in range(2):
                rows = slice(rt * 8, rt * 8 + 8)
                for b in range(2):
                    c = cnt_r[b, rows]
                    at = pl.multiple_of(l * 16 + rt * 8, 8)
                    t = tn[b, pl.ds(at, 8)]
                    up = tn[b, pl.ds(pl.multiple_of(lax.rem(at + 16, 1024), 8), 8)]
                    down = jnp.where(lev + 1.0 < c, up - t, 0.0)
                    source = (fade * (light_gain * absorb * math.exp(-j / light_decay))) * forcing[
                        b, rt * 64 + 32:rt * 64 + 40
                    ]
                    gain = diapycnal_diffusion * (down - below[rt * 2 + b]) + source
                    tpart[b, pl.ds(at, 8)] = t + jnp.where(lev < c, gain, 0.0)
                    below[rt * 2 + b] = down
        return fade * math.exp(-4.0 / light_decay), tuple(below)

    lax.fori_loop(0, strata // 4, vertical, (f32(1.0), (jnp.zeros((8, 128), f32),) * 4))
    for rt in range(2):
        rows = slice(rt * 8, rt * 8 + 8)
        for b in range(2):
            tpart[b, rows] = tpart[b, rows] + jnp.where(
                cnt_r[b, rows] > 0.5, heat_gain * forcing[b, rt * 64 + 24:rt * 64 + 32], 0.0
            )

    mn, vn = wide_row(mn_r, 23)[two], wide_row(sn_r, 23)[two]
    for q in range(8):
        part = slice(q * 8, q * 8 + 8)
        both = tv[0, part, 0:256] + tv[23, part, 0:256]
        flow[part, 0:256] = jnp.where(level[two] + float(q * 8) < mn, vn * both, 0.0)

    def advect_row(r, _):
        me, mn = wide_row(me_r, r), wide_row(mn_r, r)[two]
        ve, vn = wide_row(se_r, r), wide_row(sn_r, r)[two]
        for q in range(8):
            part = slice(q * 8, q * 8 + 8)
            lev = level + float(q * 8)
            t = tv[r, part]
            fe = jnp.where(lev < me, ve * (t + east(t)), 0.0)
            fn = jnp.where(lev[two] < mn, vn * (t[two] + tv[r + 1, part, 0:256]), 0.0)
            change = mix[r, part] + (fe - west(fe))[two] + fn - flow[part, 0:256]
            flow[part, 0:256] = fn
            for b in range(2):
                at = pl.ds(q * 128 + r, 8, stride=16)
                tnew[b, at, :] = tpart[b, at, :] + change[:, b * 128:b * 128 + 128]
        return 0

    lax.fori_loop(0, 16, advect_row, 0)

    s_s.wait_recv()
    s_n.wait_recv()

    def from_bands(s):
        part = slice(s * 8, s * 8 + 8)
        from_south = jnp.where(keep_south, rtable[0, part], 0.0)
        from_north = jnp.where(keep_north, rtable[1, part], 0.0)
        return table[1, part] + from_south + from_north

    factor = (1 - flags[...]).astype(f32) / jnp.maximum(from_bands(4), area_floor)
    for s in range(4):
        o_skin[s * 8:s * 8 + 8] = from_bands(s) * factor
    for c in sends:
        c.wait_send()


def deliver(height, zonal, meridional, thermal, skin, h_out, u_out, v_out, t_out, skin_out, sem):
    rows = t_out.shape[0]
    copies = [(height, h_out), (zonal, u_out), (meridional, v_out), (skin, skin_out)]
    copies += [(thermal.at[b, pl.ds(0, rows)], t_out.at[:, pl.ds(b * 128, 128)]) for b in range(2)]
    copies = [pltpu.make_async_copy(a, b, sem.at[i]) for i, (a, b) in enumerate(copies)]
    for c in copies:
        c.start()
    for c in copies:
        c.wait()


def shards(
    free_elevation, zonal_volume_carriage, meridional_volume_carriage, thermal_field, flooded_strata_number,
    aerial_exchanges, aerial_terrain_flags, donor_tile_number, donor_point_number, pairing_coefficients,
):
    strata = thermal_field.shape[0]
    vmem = pltpu.VMEM
    anywhere = pl.BlockSpec(memory_space=pl.ANY)
    far = pl.BlockSpec(memory_space=pltpu.HBM)
    local = pl.BlockSpec(memory_space=pltpu.VMEM)
    results = pl.pallas_call(
        kernel,
        out_shape=(vmem((16, 256), f32),) * 3 + (vmem((2, 1024, 128), f32), vmem((32, 128), f32)),
        in_specs=[far] * 10,
        out_specs=(local,) * 5,
        scratch_shapes=[
            vmem((5, 16, 256), f32), vmem((16, 256), jnp.int32), vmem((2, 1024, 128), f32), vmem((40, 128), f32),
            vmem((8, 128), jnp.int32), vmem((2, 64, 128), jnp.int32), vmem((2, 64, 128), f32),
            vmem((4, 2, 16), jnp.int32), vmem((8, 128), f32), vmem((40, 128), f32), vmem((2, 40, 128), f32),
            vmem((16, 128), f32), vmem((16, 128), f32), vmem((16, 128), f32), vmem((16, 128), f32),
            vmem((4, 8, 128), f32), vmem((2, 5, 8, 256), f32),
            vmem((24, 64, 384), f32), vmem((2, 16, 128), f32), vmem((16, 128), f32), vmem((16, 128), f32),
            vmem((4, 16, 128), f32),
            vmem((2, 128, 128), f32), vmem((16, 128), f32), vmem((16, 128), f32), vmem((16, 128), f32),
            vmem((16, 128), f32), vmem((4, 8, 128), f32), vmem((2, 2, 24, 128), f32),
            vmem((3, 24, 128), f32), vmem((3, 24, 128), f32), vmem((3, 24, 128), f32), vmem((3, 24, 128), f32),
            vmem((3, 24, 128), f32),
            vmem((24, 64, 384), f32), vmem((16, 64, 256), f32), vmem((2, 1024, 128), f32), vmem((64, 384), f32),
            vmem((128, 128), bf16), vmem((32, 128), bf16), vmem((256, 128), f32), vmem((1024, 128), f32),
            vmem((3, 40, 128), f32), vmem((2, 40, 128), f32), vmem((16, 256), f32),
            pltpu.SemaphoreType.DMA((14,)),
            pltpu.SemaphoreType.DMA((28,)), pltpu.SemaphoreType.DMA((28,)),
        ],
        compiler_params=pltpu.CompilerParams(collective_id=0, has_side_effects=True, vmem_limit_bytes=65929216),
    )(
        free_elevation, zonal_volume_carriage, meridional_volume_carriage, thermal_field.reshape(strata * 16, 256),
        flooded_strata_number, aerial_exchanges.reshape(40, 128), aerial_terrain_flags, donor_tile_number.swapaxes(1, 2),
        donor_point_number.reshape(64, 256), pairing_coefficients.reshape(64, 256),
    )
    plane = jax.ShapeDtypeStruct((16, 256), f32)
    h, u, v, t, skin = pl.pallas_call(
        deliver,
        out_shape=(plane,) * 3 + (jax.ShapeDtypeStruct((strata * 16, 256), f32), jax.ShapeDtypeStruct((32, 128), f32)),
        in_specs=[local] * 5,
        out_specs=(anywhere,) * 5,
        scratch_shapes=[pltpu.SemaphoreType.DMA((6,))],
        compiler_params=pltpu.CompilerParams(vmem_limit_bytes=8 << 20),
    )(*results)
    return h, u, v, t.reshape(strata, 16, 256), skin.reshape(4, 8, 128)


def solution(mesh):
    flat, deep = P("lat", "lon"), P(None, "lat", "lon")
    return jax.shard_map(
        shards,
        mesh=mesh,
        in_specs=(flat, flat, flat, deep, flat, deep, flat, deep, deep, deep),
        out_specs=(flat, flat, flat, deep, deep),
        check_vma=False,
    )
```

time: 218 us -> 40.2 us (0.18)
  the two profiles are of different devices: /device:TPU:57 before, /device:TPU:2 now
where the time goes in v1:
time: 40.2 us; the launch traced here: 40.1 us
  Pallas kernels  39.4 us (98%)
  between operations  0.64 us (2%)
    pallas_call x1, Pallas kernels, shards(): pl.pallas_call(kernel, out_shape=(vmem((16, 256), f32),) * 3 + (vmem((2,...  38.4 us
    pallas_call x1, Pallas kernels, shards(): pl.pallas_call(deliver, out_shape=(plane,) * 3 + (jax.ShapeDtypeStruct((s...  1.02 us

profile of v1, /device:TPU:2, one launch (start us, length us, event | category | flops | bytes accessed | tf_op | source)
XLA Modules:
  0.0 40.1 jit_solution(6805954933693615514)
XLA Ops:
  0.6 38.4 %shard_map.137 = (f32[16,256]{1,0:T(8,128)S(1)}, f32[16,256]{1,0:T(8,128)S(1)}, f32[16,256]{1,0:T(8,128)S(1)}, f32[2,1024,128]{2,1,0:T(8,128)S(1)}, f32[32,128]{1,0:T(8,128)S(1)}) custom-call(f32[16,256]{1,0:T(8,128)} %h_in.1, f32[16,256]{1,0:T(8,128)} %u_in.1, f32[16,256]{1,0:T(8,128)} %v_in.1, f32[960,256]{1,0:T(8,128)} %bitcast.7, s32[16,256]{1,0:T(8,128)} %n_in.1, ...), custom_call_target="tpu_custom_call" | custom-call | tf_op jit(solution)/shard_map/pallas_call | solution.py:553
  39.1 1.0 %shard_map.138 = (f32[16,256]{1,0:T(8,128)}, f32[16,256]{1,0:T(8,128)}, f32[16,256]{1,0:T(8,128)}, f32[960,256]{1,0:T(8,128)}, f32[32,128]{1,0:T(8,128)}) custom-call(f32[16,256]{1,0:T(8,128)S(1)} %get-tuple-element.15.height, f32[16,256]{1,0:T(8,128)S(1)} %get-tuple-element.16.zonal, f32[16,256]{1,0:T(8,128)S(1)} %get-tuple-element.17.meridional, ...), custom_call_target="tpu_custom_call" | custom-call | tf_op jit(solution)/shard_map/pallas_call | solution.py:583

commit v2 on v1

--- a/solution.py
+++ b/solution.py
@@ -20,6 +20,7 @@
 light_decay = 8.0
 depth_floor = 0.25
 area_floor = 1.0
+absorb_of = 1.0 - math.exp(-1.0 / light_decay)
 
 f32 = jnp.float32
 bf16 = jnp.bfloat16
@@ -73,10 +74,10 @@
     o_height, o_zonal, o_meridional, tnew, o_skin,
     planes, count_int, tn, flux, flags, pt, wt,
     rows_in, rows_wide, masked, rx, col_e, col_w, rcol_e, rcol_w, rdiag, rns,
-    tv, tpack, rt_e, rt_w, rt_diag,
+    tv, tpack, rt_e, rt_w, rt_diag, rt_ns, edge_mix, edge_sum,
     forcing, fcol_e, fcol_w, rf_e, rf_w, rf_diag, rf_ns,
-    cnt_r, me_r, mn_r, se_r, sn_r,
-    lap, mix, tpart, flow, rowcol, row_hot, sv, cells, table, rtable, top_part,
+    cnt_r, me_r, mn_r, se_r, sn_r, mc_r, light_r,
+    lap, mix, tpart, flow, flow2, rowcol, row_hot, sv, cells, table, rtable, top_part,
     in_sem, send_sem, recv_sem,
 ):
     strata = t_in.shape[0] // 16
@@ -89,6 +90,10 @@
     to_ne, to_nw = {"lon": le, "lat": ln}, {"lon": lw, "lat": ln}
     to_se, to_sw = {"lon": le, "lat": ls}, {"lon": lw, "lat": ls}
 
+    barrier = pltpu.get_barrier_semaphore()
+    for where in (to_n, to_s, to_e, to_w, to_ne, to_nw, to_se, to_sw):
+        pl.semaphore_signal(barrier, inc=1, device_id=where, device_id_type=pl.DeviceIdType.MESH)
+
     loads = [
         (x_in, flux), (flag_in, flags), (n_in, count_int), (h_in, planes.at[0]), (u_in, planes.at[1]),
         (v_in, planes.at[2]), (t_in.at[pl.ds(0, 16)], planes.at[4]),
@@ -101,10 +106,6 @@
     for c in load:
         c.start()
 
-    barrier = pltpu.get_barrier_semaphore()
-    for where in (to_n, to_s, to_e, to_w, to_ne, to_nw, to_se, to_sw):
-        pl.semaphore_signal(barrier, inc=1, device_id=where, device_id_type=pl.DeviceIdType.MESH)
-
     sends = []
 
     def send(src, dst, where):
@@ -143,6 +144,121 @@
         return planes[p, rt * 8:rt * 8 + 8, b * 128:b * 128 + 128]
 
     pack_columns(plane_tile, 5, col_e, col_w)
+
+    half = lax.shift_right_logical(lane, 1)
+
+    def do_turn():
+        load[12].wait()
+        load[13].wait()
+        for b in range(2):
+            tn[b, strata * 16:] = jnp.zeros((64 * 16 - strata * 16, 128), f32)
+
+        def turn(r, carry):
+            carry = list(carry)
+            for q in range(8):
+                g, q4 = q // 4, q % 4
+                here = half == r + 16 * q4
+                t0 = tn[0, pl.ds(q * 128 + r, 8, stride=16), :]
+                t1 = tn[1, pl.ds(q * 128 + r, 8, stride=16), :]
+                tv[r, q * 8:q * 8 + 8, 0:128] = t0
+                tv[r, q * 8:q * 8 + 8, 128:256] = t1
+                at = 2 * r + 32 * q4
+                carry[g] = jnp.where(here, pltpu.roll(t1, lax.rem(at + 2, 128), 1), carry[g])
+                carry[2 + g] = jnp.where(here, pltpu.roll(t0, at, 1), carry[2 + g])
+            return tuple(carry)
+
+        packs = lax.fori_loop(0, 16, turn, (jnp.zeros((8, 128), f32),) * 4, unroll=4)
+        for i in range(4):
+            tpack[i // 2, (i % 2) * 8:(i % 2) * 8 + 8] = packs[i]
+        for i in range(2):
+            packed = jnp.zeros((8, 128), f32)
+            for r in range(16):
+                row = jnp.broadcast_to(planes[3, r:r + 1, (1 - i) * 128:(1 - i) * 128 + 128], (8, 128))
+                packed = jnp.where(half == r, roll(row, 2 * r + 2 * (1 - i), 1), packed)
+            tpack[i, 16:24] = spread_groups(packed)
+
+    def spread_groups(x):
+        x = jnp.where(lane < 32, x, 0.0)
+        x = x + roll(x, 32, 1)
+        return x + roll(x, 64, 1)
+
+    two = (slice(None), slice(0, 256))
+    level = subs((8, 256)).astype(f32)
+
+    def own_row(ref, r):
+        return jnp.concatenate([jnp.broadcast_to(ref[b, pl.ds(r, 1), :], (8, 128)) for b in range(2)], axis=1)
+
+    def start_flow(dst, src, r, rn):
+        mn = own_row(mn_r, r)
+        for q in range(8):
+            part = slice(q * 8, q * 8 + 8)
+            dst[part] = jnp.where(level + float(q * 8) < mn, src[rn, part] - src[r, part], 0.0)
+
+    def lap_row(r, _):
+        rn = lax.rem(r + 1, 24)
+        me, mn = own_row(mc_r, r), own_row(mn_r, r)
+        for q in range(8):
+            part = slice(q * 8, q * 8 + 8)
+            lev = level + float(q * 8)
+            t = tv[r, part]
+            fe = jnp.where(lev < me, east(t) - t, 0.0)
+            fn = jnp.where(lev < mn, tv[rn, part] - t, 0.0)
+            lap[r, part] = fe - west(fe) + fn - flow[part]
+            flow[part] = fn
+        return 0
+
+    def mix_row(r, _):
+        me, mn = own_row(mc_r, r), own_row(mn_r, r)
+        for q in range(8):
+            part = slice(q * 8, q * 8 + 8)
+            lev = level + float(q * 8)
+            t = lap[r, part]
+            fe = jnp.where(lev < me, east(t) - t, 0.0)
+            fn = jnp.where(lev < mn, lap[r + 1, part] - t, 0.0)
+            mix[r, part] = (-mixing_fourth) * (fe - west(fe) + fn - flow2[part])
+            flow2[part] = fn
+        return 0
+
+    def do_inner():
+        start_flow(flow, tv, 0, 1)
+        lax.fori_loop(1, 15, lap_row, 0)
+        start_flow(flow2, lap, 1, 2)
+        lax.fori_loop(2, 14, mix_row, 0)
+
+    def do_vertical():
+        def vertical(i, below):
+            below = list(below)
+            for j in range(4):
+                l = i * 4 + j
+                lev = l.astype(f32)
+                for rt in range(2):
+                    for b in range(2):
+                        c = planes[3, rt * 8:rt * 8 + 8, b * 128:b * 128 + 128]
+                        at = pl.multiple_of(l * 16 + rt * 8, 8)
+                        t = tn[b, pl.ds(at, 8)]
+                        up = tn[b, pl.ds(pl.multiple_of(lax.rem(at + 16, 1024), 8), 8)]
+                        down = jnp.where(lev + 1.0 < c, up - t, 0.0)
+                        gain = diapycnal_diffusion * (down - below[rt * 2 + b])
+                        tpart[b, pl.ds(at, 8)] = t + jnp.where(lev < c, gain, 0.0)
+                        below[rt * 2 + b] = down
+            return tuple(below)
+
+        lax.fori_loop(0, strata // 4, vertical, (jnp.zeros((8, 128), f32),) * 4)
+
+    c_own = planes[3]
+    c_east = jnp.where(lanes((16, 256)) == 255, 0.0, jnp.minimum(c_own, east(c_own)))
+    c_north = jnp.minimum(c_own, north(c_own))
+    for b in range(2):
+        mc_r[b, 0:16] = c_east[:, b * 128:b * 128 + 128]
+        mn_r[b, 0:16] = c_north[:, b * 128:b * 128 + 128]
+
+    early = lax.rem(lon, n_lon // 2) < n_lon // 4
+
+    @pl.when(early)
+    def _():
+        do_turn()
+        do_vertical()
+        do_inner()
 
     pl.semaphore_wait(barrier, 8)
 
@@ -172,31 +288,9 @@
     row_hot[...] = hot[0:32].astype(bf16)
     rowcol[...] = jnp.transpose(hot).astype(bf16)
 
-    load[12].wait()
-    load[13].wait()
-    pad = 64 * 16 - strata * 16
-    for b in range(2):
-        tn[b, strata * 16:] = jnp.zeros((pad, 128), f32)
-
-    half = lax.shift_right_logical(lane, 1)
-
-    def turn(r, carry):
-        carry = list(carry)
-        for q in range(8):
-            g, q4 = q // 4, q % 4
-            here = half == r + 16 * q4
-            t0 = tn[0, pl.ds(q * 128 + r, 8, stride=16), :]
-            t1 = tn[1, pl.ds(q * 128 + r, 8, stride=16), :]
-            tv[r, q * 8:q * 8 + 8, 0:128] = t0
-            tv[r, q * 8:q * 8 + 8, 128:256] = t1
-            at = 2 * r + 32 * q4
-            carry[g] = jnp.where(here, pltpu.roll(t1, lax.rem(at + 2, 128), 1), carry[g])
-            carry[2 + g] = jnp.where(here, pltpu.roll(t0, at, 1), carry[2 + g])
-        return tuple(carry)
-
-    packs = lax.fori_loop(0, 16, turn, (jnp.zeros((8, 128), f32),) * 4, unroll=4)
-    for i in range(4):
-        tpack[i // 2, (i % 2) * 8:(i % 2) * 8 + 8] = packs[i]
+    @pl.when(jnp.logical_not(early))
+    def _():
+        do_turn()
 
     t_copies = [
         send(tpack.at[0], rt_w, to_e),
@@ -205,12 +299,18 @@
         send(tpack.at[1], rt_diag.at[2], to_nw),
         send(tpack.at[0], rt_diag.at[1], to_se),
         send(tpack.at[1], rt_diag.at[0], to_sw),
-        send(tv.at[pl.ds(14, 2), :, pl.ds(0, 256)], tv.at[pl.ds(22, 2), :, pl.ds(0, 256)], to_n),
-        send(tv.at[pl.ds(0, 2), :, pl.ds(0, 256)], tv.at[pl.ds(16, 2), :, pl.ds(0, 256)], to_s),
+        send(tv.at[pl.ds(14, 2)], tv.at[pl.ds(22, 2)], to_n),
+        send(tv.at[pl.ds(0, 2)], tv.at[pl.ds(16, 2)], to_s),
+        send(tpack, rt_ns.at[1], to_n),
+        send(tpack, rt_ns.at[0], to_s),
     ]
 
     for i in range(7, 11):
         load[i].wait()
+
+    @pl.when(jnp.logical_not(early))
+    def _():
+        do_vertical()
 
     x_n.wait_recv()
     x_s.wait_recv()
@@ -291,6 +391,9 @@
     put(cnt_r, count)
     put(me_r, min_e)
     put(mn_r, min_n)
+    closed = jnp.where(lanes((24, 384)) == 255, 0.0, min_e)
+    for b in range(2):
+        mc_r[b] = closed[:, b * 128:b * 128 + 128]
 
     def plane_laplace(field):
         fe = jnp.where(whole(me_r) > 0.5, east(field) - field, 0.0)
@@ -306,7 +409,8 @@
         )
 
     heat, light = own_forcing(3), own_forcing(4)
-    absorb = 1.0 - math.exp(-1.0 / light_decay)
+    for b in range(2):
+        light_r[b] = (light_gain * absorb_of) * light[:, b * 128:b * 128 + 128]
     t_own = planes[4]
     t_next = jnp.concatenate([tn[0, 16:32], tn[1, 16:32]], axis=1)
     top_part[...] = (
@@ -314,7 +418,7 @@
         + wet_own
         * (
             diapycnal_diffusion * jnp.where(own_part(cnt_r) > 1.5, t_next - t_own, 0.0)
-            + light_gain * absorb * light
+            + light_gain * absorb_of * light
             + heat_gain * heat
         )
         - mixing_fourth * top_mix
@@ -323,69 +427,84 @@
     for c in t_copies:
         c.wait_recv()
 
-    def unpack(r, _):
-        for q in range(8):
-            g, q4 = q // 4, q % 4
-            at = 2 * r + 32 * q4
-            e = pltpu.roll(rt_e[g * 8:g * 8 + 8], lax.rem(256 - at, 128), 1)
-            w = pltpu.roll(rt_w[g * 8:g * 8 + 8], lax.rem(254 - at, 128), 1)
-            tv[r, q * 8:q * 8 + 8, 256:384] = jnp.where(lane < 64, e, w)
-        return 0
-
-    lax.fori_loop(0, 16, unpack, 0, unroll=4)
-    for row, r, i in ((16, 0, 0), (23, 15, 2)):
-        for q in range(8):
-            g, q4 = q // 4, q % 4
-            at = 2 * r + 32 * q4
-            e = roll(rt_diag[i, g * 8:g * 8 + 8], -at, 1)
-            w = roll(rt_diag[i + 1, g * 8:g * 8 + 8], 126 - at, 1)
-            tv[row, q * 8:q * 8 + 8, 256:384] = jnp.where(lane < 64, e, w)
-
-    level = subs((8, 384)).astype(f32)
-
-    def wide_row(ref, r):
-        return jnp.concatenate([jnp.broadcast_to(ref[b, pl.ds(r, 1), :], (8, 128)) for b in range(3)], axis=1)
-
-    me = wide_row(mn_r, 22)
-    for q in range(8):
-        part = slice(q * 8, q * 8 + 8)
-        flow[part] = jnp.where(level + float(q * 8) < me, tv[23, part] - tv[22, part], 0.0)
-
-    def lap_row(i, _):
-        r, rn = lax.rem(i + 23, 24), lax.rem(i, 24)
-        me, mn = wide_row(me_r, r), wide_row(mn_r, r)
-        for q in range(8):
-            part = slice(q * 8, q * 8 + 8)
-            lev = level + float(q * 8)
-            t = tv[r, part]
-            fe = jnp.where(lev < me, east(t) - t, 0.0)
-            fn = jnp.where(lev < mn, tv[rn, part] - t, 0.0)
-            lap[r, part] = fe - west(fe) + fn - flow[part]
-            flow[part] = fn
-        return 0
-
-    lax.fori_loop(0, 18, lap_row, 0)
-
-    two = (slice(None), slice(0, 256))
-    mn = wide_row(mn_r, 23)[two]
-    for q in range(8):
-        part = slice(q * 8, q * 8 + 8)
-        rise = lap[0, part, 0:256] - lap[23, part, 0:256]
-        flow[part, 0:256] = jnp.where(level[two] + float(q * 8) < mn, rise, 0.0)
-
-    def mix_row(r, _):
-        me, mn = wide_row(me_r, r), wide_row(mn_r, r)[two]
-        for q in range(8):
-            part = slice(q * 8, q * 8 + 8)
-            lev = level + float(q * 8)
-            t = lap[r, part]
-            fe = jnp.where(lev < me, east(t) - t, 0.0)
-            fn = jnp.where(lev[two] < mn, lap[r + 1, part, 0:256] - t[two], 0.0)
-            mix[r, part] = (-mixing_fourth) * ((fe - west(fe))[two] + fn - flow[part, 0:256])
-            flow[part, 0:256] = fn
-        return 0
-
-    lax.fori_loop(0, 16, mix_row, 0)
+    @pl.when(jnp.logical_not(early))
+    def _():
+        do_inner()
+
+    lax.fori_loop(15, 17, lap_row, 0)
+    start_flow(flow, tv, 22, 23)
+    lax.fori_loop(0, 2, lambda i, _: lap_row(lax.rem(i + 23, 24), 0), 0)
+    lax.fori_loop(14, 16, mix_row, 0)
+    start_flow(flow2, lap, 23, 0)
+    lax.fori_loop(0, 2, mix_row, 0)
+
+    odd = (lane & 1) == 1
+    group_lane = lane & 31
+    keep_s, keep_n = keep_south, keep_north
+
+    def edge(side):
+        beside = rt_e if side == 0 else rt_w
+        diag_n, diag_s = (rt_diag.at[0], rt_diag.at[2]) if side == 0 else (rt_diag.at[1], rt_diag.at[3])
+
+        def join(own_pack, other):
+            return jnp.where(odd, own_pack, other) if side == 0 else jnp.where(odd, other, own_pack)
+
+        def shift_out(own_pack, other):
+            return jnp.where(odd, roll(other, 1, 1), roll(other, -1, 1)) if side == 0 else jnp.where(
+                odd, roll(other, 1, 1), roll(other, -1, 1)
+            )
+
+        def shift_in(own_pack, other):
+            return jnp.where(odd, roll(own_pack, 1, 1), roll(own_pack, -1, 1))
+
+        def up(x, x_n):
+            return jnp.where(group_lane >= 30, roll(x_n, 30, 1), roll(x, -2, 1))
+
+        def down(x, x_s):
+            return jnp.where(group_lane < 2, roll(x_s, -30, 1), roll(x, 2, 1))
+
+        mine = jnp.logical_not(odd) if side == 1 else odd
+        back = 1 if side == 0 else -1
+        rows = slice(16, 24)
+        c = join(tpack[side, rows], beside[rows])
+        c_out, c_in = shift_out(tpack[side, rows], beside[rows]), shift_in(tpack[side, rows], beside[rows])
+        cn_pack = jnp.where(keep_n, join(rt_ns[0, side, rows], diag_n[rows]), 0.0)
+        cs_pack = jnp.where(keep_s, join(rt_ns[1, side, rows], diag_s[rows]), 0.0)
+        cn_out = jnp.where(keep_n, shift_out(rt_ns[0, side, rows], diag_n[rows]), 0.0)
+        cs_out = jnp.where(keep_s, shift_out(rt_ns[1, side, rows], diag_s[rows]), 0.0)
+        m_out, m_in = jnp.minimum(c, c_out), jnp.minimum(c, c_in)
+        m_n, m_s = jnp.minimum(c, up(c, cn_pack)), jnp.minimum(c, down(c, cs_pack))
+        m_n_out, m_s_out = jnp.minimum(cn_pack, cn_out), jnp.minimum(cs_pack, cs_out)
+        for g in range(2):
+            part = slice(g * 8, g * 8 + 8)
+            lev = (sub + 8 * (4 * g + lax.shift_right_logical(lane, 5))).astype(f32)
+            own_pack, other = tpack[side, part], beside[part]
+            own_n, other_n = rt_ns[0, side, part], diag_n[part]
+            own_s, other_s = rt_ns[1, side, part], diag_s[part]
+            z = join(own_pack, other)
+            z_n, z_s = join(own_n, other_n), join(own_s, other_s)
+            z_out = shift_out(own_pack, other)
+            flux_out = jnp.where(lev < m_out, z_out - z, 0.0)
+            flux_in = jnp.where(lev < m_in, shift_in(own_pack, other) - z, 0.0)
+            flux_n = jnp.where(lev < m_n, up(z, z_n) - z, 0.0)
+            flux_s = jnp.where(lev < m_s, down(z, z_s) - z, 0.0)
+            full = flux_out + flux_in + flux_n + flux_s
+            missing = jnp.where(mine, flux_out, 0.0)
+            missing_n = jnp.where(lev < m_n_out, shift_out(own_n, other_n) - z_n, 0.0)
+            missing_s = jnp.where(lev < m_s_out, shift_out(own_s, other_s) - z_s, 0.0)
+            inward = jnp.where(lev < m_in, missing, 0.0)
+            change = (
+                jnp.where(lev < m_out, roll(full, back, 1) - full, 0.0)
+                - inward
+                + jnp.where(lev < m_n, up(missing, missing_n) - missing, 0.0)
+                + jnp.where(lev < m_s, down(missing, missing_s) - missing, 0.0)
+            )
+            change = jnp.where(mine, change, roll(inward, -back, 1))
+            edge_mix[side, part] = (-mixing_fourth) * change
+            edge_sum[side, part] = jnp.where(mine & (lev < m_out), z_out + z, 0.0)
+
+    edge(0)
+    edge(1)
 
     for c in f_copies:
         c.wait_recv()
@@ -430,19 +549,27 @@
 
     cell_id = lax.broadcasted_iota(jnp.int32, (128, 128), 0).astype(f32).astype(bf16)
 
+    wide_id = jnp.concatenate([cell_id, cell_id], axis=1)
+    blank = jnp.zeros((16, 128), bf16)
+
     def spread(r, _):
-        for b in range(2):
-            value = sv[pl.ds(pl.multiple_of(r * 16 + b * 8, 8), 8), :]
-            for k in range(4):
-                share = value * wt[b, pl.ds(k * 16 + r, 1), :]
+        value = sv[pl.ds(pl.multiple_of(r * 16, 16), 16), :]
+        for k in range(4):
+            parts, points = [], []
+            for b in range(2):
+                share = value[b * 8:b * 8 + 8] * wt[b, pl.ds(k * 16 + r, 1), :]
                 high = share.astype(bf16)
                 low = (share - high.astype(f32)).astype(bf16)
-                point = pt[b, pl.ds(k * 16 + r, 1), :].astype(f32).astype(bf16)
-                by_cell = lax.dot_general(
-                    jnp.concatenate([high, low], axis=0), jnp.where(cell_id == point, bf16(1), bf16(0)),
-                    (((1,), (1,)), ((), ())), preferred_element_type=f32,
-                )
-                cells[pl.ds((k * 2 + b) * 16 + r, 8, stride=128), :] = by_cell[0:8] + by_cell[8:16]
+                parts.append(jnp.concatenate([high, low], axis=0))
+                points.append(pt[b, pl.ds(k * 16 + r, 1), :].astype(f32).astype(bf16))
+            left = jnp.concatenate(
+                [jnp.concatenate([parts[0], blank], axis=1), jnp.concatenate([blank, parts[1]], axis=1)], axis=0
+            )
+            match = jnp.where(wide_id == jnp.concatenate(points, axis=1), bf16(1), bf16(0))
+            by_cell = lax.dot_general(left, match, (((1,), (1,)), ((), ())), preferred_element_type=f32)
+            for b in range(2):
+                both = by_cell[b * 16:b * 16 + 8] + by_cell[b * 16 + 8:b * 16 + 16]
+                cells[pl.ds((k * 2 + b) * 16 + r, 8, stride=128), :] = both
         return 0
 
     lax.fori_loop(0, 16, spread, 0, unroll=2)
@@ -460,59 +587,55 @@
     s_s = send(table.at[0], rtable.at[1], to_s)
     s_n = send(table.at[2], rtable.at[0], to_n)
 
-    def vertical(i, carry):
-        fade, below = carry
-        below = list(below)
-        for j in range(4):
-            l = i * 4 + j
-            lev = (l + 0).astype(f32)
-            for rt in range(2):
-                rows = slice(rt * 8, rt * 8 + 8)
-                for b in range(2):
-                    c = cnt_r[b, rows]
-                    at = pl.multiple_of(l * 16 + rt * 8, 8)
-                    t = tn[b, pl.ds(at, 8)]
-                    up = tn[b, pl.ds(pl.multiple_of(lax.rem(at + 16, 1024), 8), 8)]
-                    down = jnp.where(lev + 1.0 < c, up - t, 0.0)
-                    source = (fade * (light_gain * absorb * math.exp(-j / light_decay))) * forcing[
-                        b, rt * 64 + 32:rt * 64 + 40
-                    ]
-                    gain = diapycnal_diffusion * (down - below[rt * 2 + b]) + source
-                    tpart[b, pl.ds(at, 8)] = t + jnp.where(lev < c, gain, 0.0)
-                    below[rt * 2 + b] = down
-        return fade * math.exp(-4.0 / light_decay), tuple(below)
-
-    lax.fori_loop(0, strata // 4, vertical, (f32(1.0), (jnp.zeros((8, 128), f32),) * 4))
-    for rt in range(2):
-        rows = slice(rt * 8, rt * 8 + 8)
-        for b in range(2):
-            tpart[b, rows] = tpart[b, rows] + jnp.where(
-                cnt_r[b, rows] > 0.5, heat_gain * forcing[b, rt * 64 + 24:rt * 64 + 32], 0.0
-            )
-
-    mn, vn = wide_row(mn_r, 23)[two], wide_row(sn_r, 23)[two]
+    for side in range(2):
+        lane_of = (lane & 1) == 1 if side == 0 else (lane & 1) == 0
+        packed = zero
+        for r in range(16):
+            row = jnp.broadcast_to(se_r[1 + side, r:r + 1, :], (8, 128))
+            here = lane == 2 * r + 1 - side
+            packed = jnp.where(here, roll(row, 2 * r + 1 - side - 127, 1), packed)
+        speed = spread_groups(packed)
+        sign = 1.0 if side == 0 else -1.0
+        for g in range(2):
+            part = slice(g * 8, g * 8 + 8)
+            edge_mix[side, part] = edge_mix[side, part] + sign * speed * edge_sum[side, part]
+
+    mn, vn = own_row(mn_r, 23), own_row(sn_r, 23)
     for q in range(8):
         part = slice(q * 8, q * 8 + 8)
-        both = tv[0, part, 0:256] + tv[23, part, 0:256]
-        flow[part, 0:256] = jnp.where(level[two] + float(q * 8) < mn, vn * both, 0.0)
+        flow[part] = jnp.where(level + float(q * 8) < mn, vn * (tv[0, part] + tv[23, part]), 0.0)
+
+    fade = jnp.exp(-level / light_decay)
 
     def advect_row(r, _):
-        me, mn = wide_row(me_r, r), wide_row(mn_r, r)[two]
-        ve, vn = wide_row(se_r, r), wide_row(sn_r, r)[two]
+        me, mn = own_row(mc_r, r), own_row(mn_r, r)
+        ve, vn = own_row(se_r, r), own_row(sn_r, r)
+        cnt, light = own_row(cnt_r, r), own_row(light_r, r) * fade
         for q in range(8):
             part = slice(q * 8, q * 8 + 8)
             lev = level + float(q * 8)
             t = tv[r, part]
             fe = jnp.where(lev < me, ve * (t + east(t)), 0.0)
-            fn = jnp.where(lev[two] < mn, vn * (t[two] + tv[r + 1, part, 0:256]), 0.0)
-            change = mix[r, part] + (fe - west(fe))[two] + fn - flow[part, 0:256]
-            flow[part, 0:256] = fn
-            for b in range(2):
-                at = pl.ds(q * 128 + r, 8, stride=16)
-                tnew[b, at, :] = tpart[b, at, :] + change[:, b * 128:b * 128 + 128]
+            fn = jnp.where(lev < mn, vn * (t + tv[r + 1, part]), 0.0)
+            source = jnp.where(lev < cnt, light * math.exp(-q * 8 / light_decay), 0.0)
+            change = mix[r, part] + (fe - west(fe)) + (fn - flow[part]) + source
+            flow[part] = fn
+            g, at = q // 4, 2 * r + 32 * (q % 4)
+            rows = slice(g * 8, g * 8 + 8)
+            edge_w = jnp.where(lane < 2, pltpu.roll(edge_mix[1, rows], lax.rem(128 - at, 128), 1), 0.0)
+            edge_e = jnp.where(lane >= 126, pltpu.roll(edge_mix[0, rows], lax.rem(254 - at, 128), 1), 0.0)
+            at = pl.ds(q * 128 + r, 8, stride=16)
+            tnew[0, at, :] = tpart[0, at, :] + (change[:, 0:128] + edge_w)
+            tnew[1, at, :] = tpart[1, at, :] + (change[:, 128:256] + edge_e)
         return 0
 
     lax.fori_loop(0, 16, advect_row, 0)
+    for rt in range(2):
+        rows = slice(rt * 8, rt * 8 + 8)
+        for b in range(2):
+            tnew[b, rows] = tnew[b, rows] + jnp.where(
+                cnt_r[b, rows] > 0.5, heat_gain * forcing[b, rt * 64 + 24:rt * 64 + 32], 0.0
+            )
 
     s_s.wait_recv()
     s_n.wait_recv()
@@ -561,17 +684,17 @@
             vmem((4, 2, 16), jnp.int32), vmem((8, 128), f32), vmem((40, 128), f32), vmem((2, 40, 128), f32),
             vmem((16, 128), f32), vmem((16, 128), f32), vmem((16, 128), f32), vmem((16, 128), f32),
             vmem((4, 8, 128), f32), vmem((2, 5, 8, 256), f32),
-            vmem((24, 64, 384), f32), vmem((2, 16, 128), f32), vmem((16, 128), f32), vmem((16, 128), f32),
-            vmem((4, 16, 128), f32),
+            vmem((24, 64, 256), f32), vmem((2, 24, 128), f32), vmem((24, 128), f32), vmem((24, 128), f32),
+            vmem((4, 24, 128), f32), vmem((2, 2, 24, 128), f32), vmem((2, 16, 128), f32), vmem((2, 16, 128), f32),
             vmem((2, 128, 128), f32), vmem((16, 128), f32), vmem((16, 128), f32), vmem((16, 128), f32),
             vmem((16, 128), f32), vmem((4, 8, 128), f32), vmem((2, 2, 24, 128), f32),
             vmem((3, 24, 128), f32), vmem((3, 24, 128), f32), vmem((3, 24, 128), f32), vmem((3, 24, 128), f32),
-            vmem((3, 24, 128), f32),
-            vmem((24, 64, 384), f32), vmem((16, 64, 256), f32), vmem((2, 1024, 128), f32), vmem((64, 384), f32),
+            vmem((3, 24, 128), f32), vmem((2, 24, 128), f32), vmem((2, 16, 128), f32),
+            vmem((24, 64, 256), f32), vmem((16, 64, 256), f32), vmem((2, 1024, 128), f32), vmem((64, 256), f32), vmem((64, 256), f32),
             vmem((128, 128), bf16), vmem((32, 128), bf16), vmem((256, 128), f32), vmem((1024, 128), f32),
             vmem((3, 40, 128), f32), vmem((2, 40, 128), f32), vmem((16, 256), f32),
             pltpu.SemaphoreType.DMA((14,)),
-            pltpu.SemaphoreType.DMA((28,)), pltpu.SemaphoreType.DMA((28,)),
+            pltpu.SemaphoreType.DMA((30,)), pltpu.SemaphoreType.DMA((30,)),
         ],
         compiler_params=pltpu.CompilerParams(collective_id=0, has_side_effects=True, vmem_limit_bytes=65929216),
     )(

time: 40.2 us -> 34.7 us (0.86)
  the two profiles are of different devices: /device:TPU:2 before, /device:TPU:57 now
where the time goes in v2:
time: 34.7 us; the launch traced here: 34.1 us
  Pallas kernels  33.5 us (97%)
  between operations  0.64 us (2%)
    pallas_call x1, Pallas kernels, shards(): pl.pallas_call(kernel, out_shape=(vmem((16, 256), f32),) * 3 + (vmem((2,...  32.4 us
    pallas_call x1, Pallas kernels, shards(): pl.pallas_call(deliver, out_shape=(plane,) * 3 + (jax.ShapeDtypeStruct((s...  1.02 us

profile of v2, /device:TPU:57, one launch (start us, length us, event | category | flops | bytes accessed | tf_op | source)
XLA Modules:
  0.0 34.1 jit_solution(13142518002994799690)
XLA Ops:
  0.6 32.4 %shard_map.137 = (f32[16,256]{1,0:T(8,128)S(1)}, f32[16,256]{1,0:T(8,128)S(1)}, f32[16,256]{1,0:T(8,128)S(1)}, f32[2,1024,128]{2,1,0:T(8,128)S(1)}, f32[32,128]{1,0:T(8,128)S(1)}) custom-call(f32[16,256]{1,0:T(8,128)} %h_in.1, f32[16,256]{1,0:T(8,128)} %u_in.1, f32[16,256]{1,0:T(8,128)} %v_in.1, f32[960,256]{1,0:T(8,128)} %bitcast.7, s32[16,256]{1,0:T(8,128)} %n_in.1, ...), custom_call_target="tpu_custom_call" | custom-call | tf_op jit(solution)/shard_map/pallas_call | solution.py:676
  33.1 1.0 %shard_map.138 = (f32[16,256]{1,0:T(8,128)}, f32[16,256]{1,0:T(8,128)}, f32[16,256]{1,0:T(8,128)}, f32[960,256]{1,0:T(8,128)}, f32[32,128]{1,0:T(8,128)}) custom-call(f32[16,256]{1,0:T(8,128)S(1)} %get-tuple-element.15.height, f32[16,256]{1,0:T(8,128)S(1)} %get-tuple-element.16.zonal, f32[16,256]{1,0:T(8,128)S(1)} %get-tuple-element.17.meridional, ...), custom_call_target="tpu_custom_call" | custom-call | tf_op jit(solution)/shard_map/pallas_call | solution.py:706

commit v3 on v2

--- a/solution.py
+++ b/solution.py
@@ -74,10 +74,10 @@
     o_height, o_zonal, o_meridional, tnew, o_skin,
     planes, count_int, tn, flux, flags, pt, wt,
     rows_in, rows_wide, masked, rx, col_e, col_w, rcol_e, rcol_w, rdiag, rns,
-    tv, tpack, rt_e, rt_w, rt_diag, rt_ns, edge_mix, edge_sum,
+    tv, tpack, rt_e, rt_w, rt_diag, rt_ns, edge_mix, edge_sum, edge_all,
     forcing, fcol_e, fcol_w, rf_e, rf_w, rf_diag, rf_ns,
     cnt_r, me_r, mn_r, se_r, sn_r, mc_r, light_r,
-    lap, mix, tpart, flow, flow2, rowcol, row_hot, sv, cells, table, rtable, top_part,
+    lap, mix, tpart, flow, flow2, face_e, face_n, rowcol, row_hot, sv, cells, table, rtable, top_part,
     in_sem, send_sem, recv_sem,
 ):
     strata = t_in.shape[0] // 16
@@ -91,8 +91,15 @@
     to_se, to_sw = {"lon": le, "lat": ls}, {"lon": lw, "lat": ls}
 
     barrier = pltpu.get_barrier_semaphore()
-    for where in (to_n, to_s, to_e, to_w, to_ne, to_nw, to_se, to_sw):
-        pl.semaphore_signal(barrier, inc=1, device_id=where, device_id_type=pl.DeviceIdType.MESH)
+    has_n, has_s = lat < n_lat - 1, lat > 0
+
+    def greet(*places):
+        for where in places:
+            pl.semaphore_signal(barrier, inc=1, device_id=where, device_id_type=pl.DeviceIdType.MESH)
+
+    greet(to_e, to_w)
+    pl.when(has_n)(lambda: greet(to_ne, to_nw, to_n))
+    pl.when(has_s)(lambda: greet(to_se, to_sw, to_s))
 
     loads = [
         (x_in, flux), (flag_in, flags), (n_in, count_int), (h_in, planes.at[0]), (u_in, planes.at[1]),
@@ -108,15 +115,37 @@
 
     sends = []
 
-    def send(src, dst, where):
+    groups = {id(to_e): 0, id(to_w): 0, id(to_n): 1, id(to_ne): 1, id(to_nw): 1, id(to_s): 2, id(to_se): 2, id(to_sw): 2}
+
+    def plan(src, dst, where):
         i = len(sends)
         c = pltpu.make_async_remote_copy(
             src_ref=src, dst_ref=dst, send_sem=send_sem.at[i], recv_sem=recv_sem.at[i],
             device_id=where, device_id_type=pl.DeviceIdType.MESH,
         )
-        c.start()
         sends.append(c)
-        return c
+        return groups[id(where)], c
+
+    def each(copies, act, north_if, south_if):
+        def run(group):
+            for g, c in copies:
+                if g == group:
+                    act(c)
+
+        run(0)
+        if any(g == 1 for g, _ in copies):
+            pl.when(north_if)(lambda: run(1))
+        if any(g == 2 for g, _ in copies):
+            pl.when(south_if)(lambda: run(2))
+
+    def start(copies):
+        each(copies, lambda c: c.start(), has_n, has_s)
+
+    def arrive(copies):
+        each(copies, lambda c: c.wait_recv(), has_s, has_n)
+
+    def leave(copies):
+        each(copies, lambda c: c.wait_send(), has_n, has_s)
 
     lane = lanes((8, 128))
     sub = subs((8, 128))
@@ -163,7 +192,7 @@
                 tv[r, q * 8:q * 8 + 8, 0:128] = t0
                 tv[r, q * 8:q * 8 + 8, 128:256] = t1
                 at = 2 * r + 32 * q4
-                carry[g] = jnp.where(here, pltpu.roll(t1, lax.rem(at + 2, 128), 1), carry[g])
+                carry[g] = jnp.where(here, pltpu.roll(t1, (at + 2) & 127, 1), carry[g])
                 carry[2 + g] = jnp.where(here, pltpu.roll(t0, at, 1), carry[2 + g])
             return tuple(carry)
 
@@ -219,11 +248,32 @@
             flow2[part] = fn
         return 0
 
+    def sum_north(r, rn):
+        mn = own_row(mn_r, r)
+        for q in range(8):
+            part = slice(q * 8, q * 8 + 8)
+            both = tv[r, part] + tv[rn, part]
+            face_n[r, part] = jnp.where(level + float(q * 8) < mn, both, 0.0)
+
+    def sum_east(r):
+        me = own_row(mc_r, r)
+        for q in range(8):
+            part = slice(q * 8, q * 8 + 8)
+            t = tv[r, part]
+            face_e[r, part] = jnp.where(level + float(q * 8) < me, t + east(t), 0.0)
+
+    def sum_row(r, _):
+        sum_east(r)
+        sum_north(r, r + 1)
+        return 0
+
     def do_inner():
         start_flow(flow, tv, 0, 1)
         lax.fori_loop(1, 15, lap_row, 0)
         start_flow(flow2, lap, 1, 2)
         lax.fori_loop(2, 14, mix_row, 0)
+        lax.fori_loop(0, 15, sum_row, 0)
+        sum_east(15)
 
     def do_vertical():
         def vertical(i, below):
@@ -260,20 +310,21 @@
         do_vertical()
         do_inner()
 
-    pl.semaphore_wait(barrier, 8)
-
-    x_n = send(masked, rx.at[0], to_n)
-    x_s = send(masked, rx.at[1], to_s)
+    pl.semaphore_wait(barrier, 2 + 3 * has_n.astype(jnp.int32) + 3 * has_s.astype(jnp.int32))
+
+    x_copies = [plan(masked, rx.at[0], to_n), plan(masked, rx.at[1], to_s)]
+    start(x_copies)
     p_copies = [
-        send(col_e, rcol_w, to_e),
-        send(col_w, rcol_e, to_w),
-        send(col_e.at[pl.ds(8, 8)], rdiag.at[3], to_ne),
-        send(col_w.at[pl.ds(8, 8)], rdiag.at[2], to_nw),
-        send(col_e.at[pl.ds(0, 8)], rdiag.at[1], to_se),
-        send(col_w.at[pl.ds(0, 8)], rdiag.at[0], to_sw),
-        send(planes.at[:, pl.ds(8, 8)], rns.at[1], to_n),
-        send(planes.at[:, pl.ds(0, 8)], rns.at[0], to_s),
+        plan(col_e, rcol_w, to_e),
+        plan(col_w, rcol_e, to_w),
+        plan(col_e.at[pl.ds(8, 8)], rdiag.at[3], to_ne),
+        plan(col_w.at[pl.ds(8, 8)], rdiag.at[2], to_nw),
+        plan(col_e.at[pl.ds(0, 8)], rdiag.at[1], to_se),
+        plan(col_w.at[pl.ds(0, 8)], rdiag.at[0], to_sw),
+        plan(planes.at[:, pl.ds(8, 8)], rns.at[1], to_n),
+        plan(planes.at[:, pl.ds(0, 8)], rns.at[0], to_s),
     ]
+    start(p_copies)
 
     load[11].wait()
     for j in range(8):
@@ -293,31 +344,27 @@
         do_turn()
 
     t_copies = [
-        send(tpack.at[0], rt_w, to_e),
-        send(tpack.at[1], rt_e, to_w),
-        send(tpack.at[0], rt_diag.at[3], to_ne),
-        send(tpack.at[1], rt_diag.at[2], to_nw),
-        send(tpack.at[0], rt_diag.at[1], to_se),
-        send(tpack.at[1], rt_diag.at[0], to_sw),
-        send(tv.at[pl.ds(14, 2)], tv.at[pl.ds(22, 2)], to_n),
-        send(tv.at[pl.ds(0, 2)], tv.at[pl.ds(16, 2)], to_s),
-        send(tpack, rt_ns.at[1], to_n),
-        send(tpack, rt_ns.at[0], to_s),
+        plan(tpack.at[0], rt_w, to_e),
+        plan(tpack.at[1], rt_e, to_w),
+        plan(tpack.at[0], rt_diag.at[3], to_ne),
+        plan(tpack.at[1], rt_diag.at[2], to_nw),
+        plan(tpack.at[0], rt_diag.at[1], to_se),
+        plan(tpack.at[1], rt_diag.at[0], to_sw),
+        plan(tv.at[pl.ds(14, 2)], tv.at[pl.ds(22, 2)], to_n),
+        plan(tv.at[pl.ds(0, 2)], tv.at[pl.ds(16, 2)], to_s),
+        plan(tpack, rt_ns.at[1], to_n),
+        plan(tpack, rt_ns.at[0], to_s),
     ]
+    start(t_copies)
 
     for i in range(7, 11):
         load[i].wait()
 
-    @pl.when(jnp.logical_not(early))
-    def _():
-        do_vertical()
-
-    x_n.wait_recv()
-    x_s.wait_recv()
+    arrive(x_copies)
     keep_south = jnp.broadcast_to(lat, (8, 128)) > 0
     keep_north = jnp.broadcast_to(lat, (8, 128)) < n_lat - 1
     zero = jnp.zeros((8, 128), f32)
-    for f in range(5):
+    def regrid(f):
         part = slice(f * 8, f * 8 + 8)
         bands = jnp.concatenate(
             [jnp.where(keep_south, rx[0, part], 0.0), masked[part], jnp.where(keep_north, rx[1, part], 0.0), zero], axis=0
@@ -339,21 +386,28 @@
                     acc = acc + cell * wt[b, at]
                 forcing[b, rt * 64 + f * 8:rt * 64 + f * 8 + 8] = acc
 
+    for f in range(3):
+        regrid(f)
+
     def forcing_tile(f, rt, b):
         return forcing[b, rt * 64 + f * 8:rt * 64 + f * 8 + 8]
 
     pack_columns(forcing_tile, 3, fcol_e, fcol_w)
 
     f_copies = [
-        send(fcol_e, rf_w, to_e),
-        send(fcol_w, rf_e, to_w),
-        send(fcol_e.at[pl.ds(8, 8)], rf_diag.at[3], to_ne),
-        send(fcol_w.at[pl.ds(8, 8)], rf_diag.at[2], to_nw),
-        send(fcol_e.at[pl.ds(0, 8)], rf_diag.at[1], to_se),
-        send(fcol_w.at[pl.ds(0, 8)], rf_diag.at[0], to_sw),
-        send(forcing.at[:, pl.ds(64, 24)], rf_ns.at[1], to_n),
-        send(forcing.at[:, pl.ds(0, 24)], rf_ns.at[0], to_s),
+        plan(fcol_e, rf_w, to_e),
+        plan(fcol_w, rf_e, to_w),
+        plan(fcol_e.at[pl.ds(8, 8)], rf_diag.at[3], to_ne),
+        plan(fcol_w.at[pl.ds(8, 8)], rf_diag.at[2], to_nw),
+        plan(fcol_e.at[pl.ds(0, 8)], rf_diag.at[1], to_se),
+        plan(fcol_w.at[pl.ds(0, 8)], rf_diag.at[0], to_sw),
+        plan(forcing.at[:, pl.ds(64, 24)], rf_ns.at[1], to_n),
+        plan(forcing.at[:, pl.ds(0, 24)], rf_ns.at[0], to_s),
     ]
+    start(f_copies)
+
+    for f in range(3, 5):
+        regrid(f)
 
     def extended(p, tiles, ns, ce, cw, diag):
         def side(e, w):
@@ -363,13 +417,15 @@
         for rt in range(2):
             part = slice(rt * 8, rt * 8 + 8)
             rows.append(jnp.concatenate([tiles(p, rt, 0), tiles(p, rt, 1), side(ce[part], cw[part])], axis=1))
-        edge = [jnp.where(sub < 4, ns(0, p, b), ns(1, p, b)) for b in range(2)]
-        corner = jnp.where(sub < 4, side(diag[0], diag[1]), side(diag[2], diag[3]))
+        def rim(north_side, south_side):
+            return jnp.where(sub < 4, jnp.where(keep_north, north_side, 0.0), jnp.where(keep_south, south_side, 0.0))
+
+        edge = [rim(ns(0, p, b), ns(1, p, b)) for b in range(2)]
+        corner = rim(side(diag[0], diag[1]), side(diag[2], diag[3]))
         rows.append(jnp.concatenate(edge + [corner], axis=1))
         return jnp.concatenate(rows, axis=0)
 
-    for c in p_copies:
-        c.wait_recv()
+    arrive(p_copies)
 
     def plane_ns(i, p, b):
         return rns[i, p, :, b * 128:b * 128 + 128]
@@ -424,12 +480,12 @@
         - mixing_fourth * top_mix
     )
 
-    for c in t_copies:
-        c.wait_recv()
+    arrive(t_copies)
 
     @pl.when(jnp.logical_not(early))
     def _():
         do_inner()
+        do_vertical()
 
     lax.fori_loop(15, 17, lap_row, 0)
     start_flow(flow, tv, 22, 23)
@@ -437,6 +493,20 @@
     lax.fori_loop(14, 16, mix_row, 0)
     start_flow(flow2, lap, 23, 0)
     lax.fori_loop(0, 2, mix_row, 0)
+    sum_north(15, 16)
+    sum_north(23, 0)
+
+    fade = jnp.exp(-level / light_decay)
+
+    def source_row(r, _):
+        cnt, light = own_row(cnt_r, r), own_row(light_r, r) * fade
+        for q in range(8):
+            part = slice(q * 8, q * 8 + 8)
+            lit = light * math.exp(-q * 8 / light_decay)
+            mix[r, part] = mix[r, part] + jnp.where(level + float(q * 8) < cnt, lit, 0.0)
+        return 0
+
+    lax.fori_loop(0, 16, source_row, 0)
 
     odd = (lane & 1) == 1
     group_lane = lane & 31
@@ -506,8 +576,8 @@
     edge(0)
     edge(1)
 
-    for c in f_copies:
-        c.wait_recv()
+    leave(x_copies + p_copies + t_copies)
+    arrive(f_copies)
 
     def forcing_ns(i, f, b):
         return rf_ns[i, b, f * 8:f * 8 + 8]
@@ -584,8 +654,8 @@
         for band in range(3):
             table[band, s * 8:s * 8 + 8] = rows[band * 8:band * 8 + 8]
 
-    s_s = send(table.at[0], rtable.at[1], to_s)
-    s_n = send(table.at[2], rtable.at[0], to_n)
+    s_copies = [plan(table.at[0], rtable.at[1], to_s), plan(table.at[2], rtable.at[0], to_n)]
+    start(s_copies)
 
     for side in range(2):
         lane_of = (lane & 1) == 1 if side == 0 else (lane & 1) == 0
@@ -598,32 +668,26 @@
         sign = 1.0 if side == 0 else -1.0
         for g in range(2):
             part = slice(g * 8, g * 8 + 8)
-            edge_mix[side, part] = edge_mix[side, part] + sign * speed * edge_sum[side, part]
-
-    mn, vn = own_row(mn_r, 23), own_row(sn_r, 23)
+            total = edge_mix[side, part] + sign * speed * edge_sum[side, part]
+            for q4 in range(4):
+                q = g * 4 + q4
+                edge_all[side, q * 8:q * 8 + 8] = roll(total, -32 * q4 - 2 * (1 - side), 1)
+
+    vn = own_row(sn_r, 23)
     for q in range(8):
         part = slice(q * 8, q * 8 + 8)
-        flow[part] = jnp.where(level + float(q * 8) < mn, vn * (tv[0, part] + tv[23, part]), 0.0)
-
-    fade = jnp.exp(-level / light_decay)
+        flow[part] = vn * face_n[23, part]
 
     def advect_row(r, _):
-        me, mn = own_row(mc_r, r), own_row(mn_r, r)
         ve, vn = own_row(se_r, r), own_row(sn_r, r)
-        cnt, light = own_row(cnt_r, r), own_row(light_r, r) * fade
+        turn_by = (128 - 2 * r) & 127
         for q in range(8):
             part = slice(q * 8, q * 8 + 8)
-            lev = level + float(q * 8)
-            t = tv[r, part]
-            fe = jnp.where(lev < me, ve * (t + east(t)), 0.0)
-            fn = jnp.where(lev < mn, vn * (t + tv[r + 1, part]), 0.0)
-            source = jnp.where(lev < cnt, light * math.exp(-q * 8 / light_decay), 0.0)
-            change = mix[r, part] + (fe - west(fe)) + (fn - flow[part]) + source
+            fe, fn = ve * face_e[r, part], vn * face_n[r, part]
+            change = mix[r, part] + (fe - west(fe)) + (fn - flow[part])
             flow[part] = fn
-            g, at = q // 4, 2 * r + 32 * (q % 4)
-            rows = slice(g * 8, g * 8 + 8)
-            edge_w = jnp.where(lane < 2, pltpu.roll(edge_mix[1, rows], lax.rem(128 - at, 128), 1), 0.0)
-            edge_e = jnp.where(lane >= 126, pltpu.roll(edge_mix[0, rows], lax.rem(254 - at, 128), 1), 0.0)
+            edge_w = jnp.where(lane < 2, pltpu.roll(edge_all[1, part], turn_by, 1), 0.0)
+            edge_e = jnp.where(lane >= 126, pltpu.roll(edge_all[0, part], turn_by, 1), 0.0)
             at = pl.ds(q * 128 + r, 8, stride=16)
             tnew[0, at, :] = tpart[0, at, :] + (change[:, 0:128] + edge_w)
             tnew[1, at, :] = tpart[1, at, :] + (change[:, 128:256] + edge_e)
@@ -637,8 +701,8 @@
                 cnt_r[b, rows] > 0.5, heat_gain * forcing[b, rt * 64 + 24:rt * 64 + 32], 0.0
             )
 
-    s_s.wait_recv()
-    s_n.wait_recv()
+    leave(f_copies)
+    arrive(s_copies)
 
     def from_bands(s):
         part = slice(s * 8, s * 8 + 8)
@@ -649,8 +713,7 @@
     factor = (1 - flags[...]).astype(f32) / jnp.maximum(from_bands(4), area_floor)
     for s in range(4):
         o_skin[s * 8:s * 8 + 8] = from_bands(s) * factor
-    for c in sends:
-        c.wait_send()
+    leave(s_copies)
 
 
 def deliver(height, zonal, meridional, thermal, skin, h_out, u_out, v_out, t_out, skin_out, sem):
@@ -686,11 +749,13 @@
             vmem((4, 8, 128), f32), vmem((2, 5, 8, 256), f32),
             vmem((24, 64, 256), f32), vmem((2, 24, 128), f32), vmem((24, 128), f32), vmem((24, 128), f32),
             vmem((4, 24, 128), f32), vmem((2, 2, 24, 128), f32), vmem((2, 16, 128), f32), vmem((2, 16, 128), f32),
+            vmem((2, 64, 128), f32),
             vmem((2, 128, 128), f32), vmem((16, 128), f32), vmem((16, 128), f32), vmem((16, 128), f32),
             vmem((16, 128), f32), vmem((4, 8, 128), f32), vmem((2, 2, 24, 128), f32),
             vmem((3, 24, 128), f32), vmem((3, 24, 128), f32), vmem((3, 24, 128), f32), vmem((3, 24, 128), f32),
             vmem((3, 24, 128), f32), vmem((2, 24, 128), f32), vmem((2, 16, 128), f32),
             vmem((24, 64, 256), f32), vmem((16, 64, 256), f32), vmem((2, 1024, 128), f32), vmem((64, 256), f32), vmem((64, 256), f32),
+            vmem((16, 64, 256), f32), vmem((24, 64, 256), f32),
             vmem((128, 128), bf16), vmem((32, 128), bf16), vmem((256, 128), f32), vmem((1024, 128), f32),
             vmem((3, 40, 128), f32), vmem((2, 40, 128), f32), vmem((16, 256), f32),
             pltpu.SemaphoreType.DMA((14,)),

time: 34.7 us -> 34.2 us (0.986); the launches traced: 34.1 us -> 34 us
  no operation moved by 1% of the time
where the time goes in v3:
time: 34.2 us; the launch traced here: 34 us
  Pallas kernels  33.4 us (98%)
  between operations  0.64 us (2%)
    pallas_call x1, Pallas kernels, shards(): pl.pallas_call(kernel, out_shape=(vmem((16, 256), f32),) * 3 + (vmem((2,...  32.4 us
    pallas_call x1, Pallas kernels, shards(): pl.pallas_call(deliver, out_shape=(plane,) * 3 + (jax.ShapeDtypeStruct((s...  1.02 us

profile of v3, /device:TPU:57, one launch (start us, length us, event | category | flops | bytes accessed | tf_op | source)
XLA Modules:
  0.0 34.0 jit_solution(2371605180260862791)
XLA Ops:
  0.6 32.4 %shard_map.137 = (f32[16,256]{1,0:T(8,128)S(1)}, f32[16,256]{1,0:T(8,128)S(1)}, f32[16,256]{1,0:T(8,128)S(1)}, f32[2,1024,128]{2,1,0:T(8,128)S(1)}, f32[32,128]{1,0:T(8,128)S(1)}) custom-call(f32[16,256]{1,0:T(8,128)} %h_in.1, f32[16,256]{1,0:T(8,128)} %u_in.1, f32[16,256]{1,0:T(8,128)} %v_in.1, f32[960,256]{1,0:T(8,128)} %bitcast.7, s32[16,256]{1,0:T(8,128)} %n_in.1, ...), custom_call_target="tpu_custom_call" | custom-call | tf_op jit(solution)/shard_map/pallas_call | solution.py:739
  33.0 1.0 %shard_map.138 = (f32[16,256]{1,0:T(8,128)}, f32[16,256]{1,0:T(8,128)}, f32[16,256]{1,0:T(8,128)}, f32[960,256]{1,0:T(8,128)}, f32[32,128]{1,0:T(8,128)}) custom-call(f32[16,256]{1,0:T(8,128)S(1)} %get-tuple-element.15.height, f32[16,256]{1,0:T(8,128)S(1)} %get-tuple-element.16.zonal, f32[16,256]{1,0:T(8,128)S(1)} %get-tuple-element.17.meridional, ...), custom_call_target="tpu_custom_call" | custom-call | tf_op jit(solution)/shard_map/pallas_call | solution.py:771
